TPU v7x, 32 devices: a whole 2x2x4 slice. The times are simulated.
32 devices in a mesh: seq: 16 (over z, y, core), ctx: 2 (over x).
Axes of the slice: x: 2, y: 2, z: 4, core: 2. Of those that a mesh axis runs over, the one named last changes fastest.
Arguments:
- tokens: bfloat16 [16, 1024, 512], P('seq', 'ctx'), may hold values from -6 to 6
- cotangent: bfloat16 [16, 1024, 512], P('seq', 'ctx'), may hold values from -6 to 6
- attn_norm_gain: bfloat16 [512], P(('seq', 'ctx')), may hold values from 0.099609375 to 1.8984375
- attn_norm_bias: bfloat16 [512], P(('seq', 'ctx')), may hold values from -2 to 2
- mlp_norm_gain: bfloat16 [512], P(('seq', 'ctx')), may hold values from 0.099609375 to 1.8984375
- mlp_norm_bias: bfloat16 [512], P(('seq', 'ctx')), may hold values from -2 to 2
- qkv_weight: bfloat16 [786432], P(('seq', 'ctx')), may hold values from -0.25 to 0.25
- qkv_bias: bfloat16 [1536], P(('seq', 'ctx')), may hold values from -2 to 2
- dense_weight: bfloat16 [262144], P(('seq', 'ctx')), may hold values from -3 to 3
- dense_bias: bfloat16 [512], P(('seq', 'ctx')), may hold values from -2 to 2
- fc_in_weight: bfloat16 [1048576], P(('seq', 'ctx')), may hold values from -0.25 to 0.25
- fc_in_bias: bfloat16 [2048], P(('seq', 'ctx')), may hold values from -2 to 2
- fc_out_weight: bfloat16 [1048576], P(('seq', 'ctx')), may hold values from -0.125 to 0.125
- fc_out_bias: bfloat16 [512], P(('seq', 'ctx')), may hold values from -2 to 2
Outputs:
- layer_out: bfloat16 [16, 1024, 512], P('seq', 'ctx')
- grad_tokens: bfloat16 [16, 1024, 512], P('seq', 'ctx')
- grad_attn_norm_gain: float32 [512], P(('seq', 'ctx'))
- grad_attn_norm_bias: float32 [512], P(('seq', 'ctx'))
- grad_mlp_norm_gain: float32 [512], P(('seq', 'ctx'))
- grad_mlp_norm_bias: float32 [512], P(('seq', 'ctx'))
- grad_qkv_weight: float32 [786432], P(('seq', 'ctx'))
- grad_qkv_bias: float32 [1536], P(('seq', 'ctx'))
- grad_dense_weight: float32 [262144], P(('seq', 'ctx'))
- grad_dense_bias: float32 [512], P(('seq', 'ctx'))
- grad_fc_in_weight: float32 [1048576], P(('seq', 'ctx'))
- grad_fc_in_bias: float32 [2048], P(('seq', 'ctx'))
- grad_fc_out_weight: float32 [1048576], P(('seq', 'ctx'))
- grad_fc_out_bias: float32 [512], P(('seq', 'ctx'))
All inputs are finite; a program needn't handle non-finite values.
Results may differ from a plain program's by a relative error of at most 0.0096.
Values may be sent and summed in bfloat16 or wider, within the bound.
A program may use at most 128 MiB of HBM per device.

v0:
```python
import jax
import jax.numpy as jnp
from jax import lax
from jax.sharding import PartitionSpec as P

D = 512
HEADS = 8
FF = 2048


EPS = 1e-05
ROPE_BASE = 10000.0
NEG = -1e30


def layer_normalize(values, gain, bias):
    mean = jnp.mean(values, axis=-1, keepdims=True)
    centered = values - mean
    var = jnp.mean(centered * centered, axis=-1, keepdims=True)
    return centered * lax.rsqrt(var + EPS) * gain + bias


def rotate(values, cosine, sine):
    width = cosine.shape[-1]
    half = width // 2
    part = values[..., :width]
    turned = jnp.concatenate([-part[..., half:], part[..., :half]], axis=-1)
    return jnp.concatenate([part * cosine + turned * sine, values[..., width:]], axis=-1)


def gelu_exact(values):
    return jax.nn.gelu(values, approximate=False)


def matrices(mix_flat, proj_flat, expand_flat, reduce_flat):
    return (
        mix_flat.reshape(D, 3 * D),
        proj_flat.reshape(D, D),
        expand_flat.reshape(D, FF),
        reduce_flat.reshape(FF, D),
    )


def body(
    tokens,
    cotangent,
    attn_norm_gain,
    attn_norm_bias,
    mlp_norm_gain,
    mlp_norm_bias,
    qkv_weight,
    qkv_bias,
    dense_weight,
    dense_bias,
    fc_in_weight,
    fc_in_bias,
    fc_out_weight,
    fc_out_bias,
):
    (
        gain_attn,
        attention_shift,
        gain_mlp,
        shift_mlp,
        mix_flat,
        mix_bias,
        proj_flat,
        proj_bias,
        expand_flat,
        expand_bias,
        reduce_flat,
        reduce_bias,
    ) = (
        lax.all_gather(attn_norm_gain, ("seq", "ctx"), axis=0, tiled=True),
        lax.all_gather(attn_norm_bias, ("seq", "ctx"), axis=0, tiled=True),
        lax.all_gather(mlp_norm_gain, ("seq", "ctx"), axis=0, tiled=True),
        lax.all_gather(mlp_norm_bias, ("seq", "ctx"), axis=0, tiled=True),
        lax.all_gather(qkv_weight, ("seq", "ctx"), axis=0, tiled=True),
        lax.all_gather(qkv_bias, ("seq", "ctx"), axis=0, tiled=True),
        lax.all_gather(dense_weight, ("seq", "ctx"), axis=0, tiled=True),
        lax.all_gather(dense_bias, ("seq", "ctx"), axis=0, tiled=True),
        lax.all_gather(fc_in_weight, ("seq", "ctx"), axis=0, tiled=True),
        lax.all_gather(fc_in_bias, ("seq", "ctx"), axis=0, tiled=True),
        lax.all_gather(fc_out_weight, ("seq", "ctx"), axis=0, tiled=True),
        lax.all_gather(fc_out_bias, ("seq", "ctx"), axis=0, tiled=True),
    )
    mix_weight, proj_weight, expand_weight, reduce_weight = matrices(
        mix_flat, proj_flat, expand_flat, reduce_flat
    )
    shape = tokens.shape
    group = shape[1]
    width = shape[2]
    heads = HEADS
    head_dim = width // heads
    rows = tokens.reshape(group, width).astype(jnp.float32)
    attn_in, attn_norm_back = jax.vjp(
        layer_normalize, rows, gain_attn.astype(jnp.float32), attention_shift.astype(jnp.float32)
    )
    mlp_in, mlp_norm_back = jax.vjp(
        layer_normalize, rows, gain_mlp.astype(jnp.float32), shift_mlp.astype(jnp.float32)
    )
    attn_low = attn_in.astype(jnp.bfloat16)
    mlp_low = mlp_in.astype(jnp.bfloat16)
    mixed = jnp.dot(attn_low, mix_weight, preferred_element_type=jnp.float32) + mix_bias.astype(
        jnp.float32
    )
    mixed = mixed.reshape(group, heads, 3, head_dim)
    place = lax.axis_index("ctx")
    blocks_total = lax.axis_size("ctx")
    local_pos = jnp.arange(group, dtype=jnp.int32)
    query_pos = place * group + local_pos
    rot_dims = head_dim // 4
    inverse = 1.0 / ROPE_BASE ** (
        jnp.arange(0, rot_dims, 2, dtype=jnp.int32).astype(jnp.float32) / rot_dims
    )
    angles = query_pos.astype(jnp.float32)[:, None] * inverse[None, :]
    angles = jnp.concatenate([angles, angles], axis=-1)
    cosine = jnp.cos(angles)[:, None, :]
    sine = jnp.sin(angles)[:, None, :]
    scale = head_dim ** (-0.5)

    def turn(query_unrotated, key_raw):
        return (rotate(query_unrotated, cosine, sine) * scale, rotate(key_raw, cosine, sine))

    (query_f, key_f), turn_back = jax.vjp(turn, mixed[:, :, 0], mixed[:, :, 1])
    query = query_f.astype(jnp.bfloat16)
    key_own = key_f.astype(jnp.bfloat16).reshape(group, width)
    value_own = mixed[:, :, 2].astype(jnp.bfloat16).reshape(group, width)
    all_keys, all_values = (
        lax.all_gather(key_own, "ctx", axis=0, tiled=True),
        lax.all_gather(value_own, "ctx", axis=0, tiled=True),
    )
    count = place + 1

    def block(index):
        keys = lax.dynamic_slice_in_dim(all_keys, index * group, group, 0).reshape(
            group, heads, head_dim
        )
        values = lax.dynamic_slice_in_dim(all_values, index * group, group, 0).reshape(
            group, heads, head_dim
        )
        scores = jnp.einsum("qhd,khd->hqk", query, keys, preferred_element_type=jnp.float32)
        allowed = (index * group + local_pos)[None, :] <= query_pos[:, None]
        return (keys, values, scores, allowed[None])

    def max_step(index, carry):
        top, total = carry
        _, _, scores, allowed = block(index)
        new_top = jnp.maximum(top, jnp.max(jnp.where(allowed, scores, NEG), axis=-1))
        terms = jnp.where(allowed, jnp.exp(scores - new_top[:, :, None]), 0.0)
        return (new_top, total * jnp.exp(top - new_top) + jnp.sum(terms, axis=-1))

    start = (jnp.full((heads, group), NEG, jnp.float32), jnp.zeros((heads, group), jnp.float32))
    top, total = lax.fori_loop(0, count, max_step, start)
    log_total = top + jnp.log(total)

    def probs_of(scores, allowed):
        return jnp.where(allowed, jnp.exp(scores - log_total[:, :, None]), 0.0)

    def out_step(index, acc):
        _, values, scores, allowed = block(index)
        probs = probs_of(scores, allowed).astype(jnp.bfloat16)
        return acc + jnp.einsum("hqk,khd->qhd", probs, values, preferred_element_type=jnp.float32)

    heads_out = lax.fori_loop(0, count, out_step, jnp.zeros((group, heads, head_dim), jnp.float32))
    attn_out = heads_out.reshape(group, width).astype(jnp.bfloat16)
    branch_attn = jnp.dot(
        attn_out, proj_weight, preferred_element_type=jnp.float32
    ) + proj_bias.astype(jnp.float32)
    expand = jnp.dot(
        mlp_low, expand_weight, preferred_element_type=jnp.float32
    ) + expand_bias.astype(jnp.float32)
    active_rows, active_back = jax.vjp(gelu_exact, expand)
    active_low = active_rows.astype(jnp.bfloat16)
    branch_mlp = jnp.dot(
        active_low, reduce_weight, preferred_element_type=jnp.float32
    ) + reduce_bias.astype(jnp.float32)
    layer_out = (rows + branch_attn + branch_mlp).astype(jnp.bfloat16).reshape(shape)
    back_mix, back_proj, back_expand, back_reduce = (
        lax.all_gather(qkv_weight, ("seq", "ctx"), axis=0, tiled=True),
        lax.all_gather(dense_weight, ("seq", "ctx"), axis=0, tiled=True),
        lax.all_gather(fc_in_weight, ("seq", "ctx"), axis=0, tiled=True),
        lax.all_gather(fc_out_weight, ("seq", "ctx"), axis=0, tiled=True),
    )
    back_mix, back_proj, back_expand, back_reduce = matrices(
        back_mix, back_proj, back_expand, back_reduce
    )
    grad_rows = cotangent.reshape(group, width)
    grad_float = grad_rows.astype(jnp.float32)
    grad_reduce = jnp.einsum("tf,td->fd", active_low, grad_rows, preferred_element_type=jnp.float32)
    grad_out_bias = jnp.sum(grad_float, axis=0)
    grad_proj = jnp.einsum("te,td->ed", attn_out, grad_rows, preferred_element_type=jnp.float32)
    grad_active = jnp.einsum(
        "td,fd->tf", grad_rows, back_reduce, preferred_element_type=jnp.float32
    )
    grad_expand = active_back(grad_active)[0].astype(jnp.bfloat16)
    grad_expand_w = jnp.einsum(
        "td,tf->df", mlp_low, grad_expand, preferred_element_type=jnp.float32
    )
    grad_expand_b = jnp.sum(grad_expand.astype(jnp.float32), axis=0)
    grad_mlp_in = jnp.einsum(
        "tf,df->td", grad_expand, back_expand, preferred_element_type=jnp.float32
    )
    grad_heads = jnp.einsum("td,ed->te", grad_rows, back_proj, preferred_element_type=jnp.float32)
    grad_heads = grad_heads.astype(jnp.bfloat16).reshape(group, heads, head_dim)

    def delta_step(index, acc):
        _, values, scores, allowed = block(index)
        probs = probs_of(scores, allowed)
        grad_probs = jnp.einsum(
            "qhd,khd->hqk", grad_heads, values, preferred_element_type=jnp.float32
        )
        return acc + jnp.sum(probs * grad_probs, axis=-1)

    delta = lax.fori_loop(0, count, delta_step, jnp.zeros((heads, group), jnp.float32))

    def query_step(index, grad_query):
        keys, values, scores, allowed = block(index)
        probs = probs_of(scores, allowed)
        grad_probs = jnp.einsum(
            "qhd,khd->hqk", grad_heads, values, preferred_element_type=jnp.float32
        )
        grad_scores = (probs * (grad_probs - delta[:, :, None])).astype(jnp.bfloat16)
        return grad_query + jnp.einsum(
            "hqk,khd->qhd", grad_scores, keys, preferred_element_type=jnp.float32
        )

    grad_query = lax.fori_loop(
        0, count, query_step, jnp.zeros((group, heads, head_dim), jnp.float32)
    )
    all_queries, all_grad_heads = (
        lax.all_gather(query.reshape(group, width), "ctx", axis=0, tiled=True),
        lax.all_gather(grad_heads.reshape(group, width), "ctx", axis=0, tiled=True),
    )
    gathered_log_sums, all_delta = (
        lax.all_gather(jnp.transpose(log_total), "ctx", axis=0, tiled=True),
        lax.all_gather(jnp.transpose(delta), "ctx", axis=0, tiled=True),
    )
    keys_mine = key_own.reshape(group, heads, head_dim)
    values_mine = value_own.reshape(group, heads, head_dim)

    def owner_step(index, carry):
        key_acc, value_accumulator = carry
        queries = lax.dynamic_slice_in_dim(all_queries, index * group, group, 0).reshape(
            group, heads, head_dim
        )
        outer_grads = lax.dynamic_slice_in_dim(all_grad_heads, index * group, group, 0).reshape(
            group, heads, head_dim
        )
        lse_rows = jnp.transpose(
            lax.dynamic_slice_in_dim(gathered_log_sums, index * group, group, 0)
        )
        delta_rows = jnp.transpose(lax.dynamic_slice_in_dim(all_delta, index * group, group, 0))
        scores = jnp.einsum("qhd,khd->hqk", queries, keys_mine, preferred_element_type=jnp.float32)
        allowed = (query_pos[None, :] <= (index * group + local_pos)[:, None])[None]
        probs = jnp.where(allowed, jnp.exp(scores - lse_rows[:, :, None]), 0.0)
        grad_probs = jnp.einsum(
            "qhd,khd->hqk", outer_grads, values_mine, preferred_element_type=jnp.float32
        )
        grad_scores = (probs * (grad_probs - delta_rows[:, :, None])).astype(jnp.bfloat16)
        key_acc = key_acc + jnp.einsum(
            "hqk,qhd->khd", grad_scores, queries, preferred_element_type=jnp.float32
        )
        value_accumulator = value_accumulator + jnp.einsum(
            "hqk,qhd->khd",
            probs.astype(jnp.bfloat16),
            outer_grads,
            preferred_element_type=jnp.float32,
        )
        return (key_acc, value_accumulator)

    empty_heads = jnp.zeros((group, heads, head_dim), jnp.float32)
    own_key_grad, own_value_grad = lax.fori_loop(
        place, blocks_total, owner_step, (empty_heads, empty_heads)
    )
    grad_query_raw, grad_key_raw = turn_back((grad_query, own_key_grad))
    grad_mixed = jnp.stack([grad_query_raw, grad_key_raw, own_value_grad], axis=2)
    grad_mixed = grad_mixed.reshape(group, 3 * width).astype(jnp.bfloat16)
    grad_mix_w = jnp.einsum("td,te->de", attn_low, grad_mixed, preferred_element_type=jnp.float32)
    grad_mix_b = jnp.sum(grad_mixed.astype(jnp.float32), axis=0)
    grad_attn_in = jnp.einsum("te,de->td", grad_mixed, back_mix, preferred_element_type=jnp.float32)
    input_attn, gain_attn_grad, shift_attn_grad = attn_norm_back(grad_attn_in)
    input_mlp, gain_mlp_grad, shift_mlp_grad = mlp_norm_back(grad_mlp_in)
    grad_tokens = (grad_float + input_attn + input_mlp).astype(jnp.bfloat16).reshape(shape)
    sums = (
        lax.psum_scatter(gain_attn_grad, ("seq", "ctx"), scatter_dimension=0, tiled=True),
        lax.psum_scatter(shift_attn_grad, ("seq", "ctx"), scatter_dimension=0, tiled=True),
        lax.psum_scatter(gain_mlp_grad, ("seq", "ctx"), scatter_dimension=0, tiled=True),
        lax.psum_scatter(shift_mlp_grad, ("seq", "ctx"), scatter_dimension=0, tiled=True),
        lax.psum_scatter(grad_mix_w.reshape(-1), ("seq", "ctx"), scatter_dimension=0, tiled=True),
        lax.psum_scatter(grad_mix_b, ("seq", "ctx"), scatter_dimension=0, tiled=True),
        lax.psum_scatter(grad_proj.reshape(-1), ("seq", "ctx"), scatter_dimension=0, tiled=True),
        lax.psum_scatter(grad_out_bias, ("seq", "ctx"), scatter_dimension=0, tiled=True),
        lax.psum_scatter(
            grad_expand_w.reshape(-1), ("seq", "ctx"), scatter_dimension=0, tiled=True
        ),
        lax.psum_scatter(grad_expand_b, ("seq", "ctx"), scatter_dimension=0, tiled=True),
        lax.psum_scatter(grad_reduce.reshape(-1), ("seq", "ctx"), scatter_dimension=0, tiled=True),
        lax.psum_scatter(grad_out_bias, ("seq", "ctx"), scatter_dimension=0, tiled=True),
    )
    return (
        layer_out,
        grad_tokens,
        sums[0],
        sums[1],
        sums[2],
        sums[3],
        sums[4],
        sums[5],
        sums[6],
        sums[7],
        sums[8],
        sums[9],
        sums[10],
        sums[11],
    )


def solution(mesh):
    return jax.shard_map(
        body,
        mesh=mesh,
        in_specs=(
            P("seq", "ctx", None),
            P("seq", "ctx", None),
            P(("seq", "ctx")),
            P(("seq", "ctx")),
            P(("seq", "ctx")),
            P(("seq", "ctx")),
            P(("seq", "ctx")),
            P(("seq", "ctx")),
            P(("seq", "ctx")),
            P(("seq", "ctx")),
            P(("seq", "ctx")),
            P(("seq", "ctx")),
            P(("seq", "ctx")),
            P(("seq", "ctx")),
        ),
        out_specs=(
            P("seq", "ctx", None),
            P("seq", "ctx", None),
            P(("seq", "ctx")),
            P(("seq", "ctx")),
            P(("seq", "ctx")),
            P(("seq", "ctx")),
            P(("seq", "ctx")),
            P(("seq", "ctx")),
            P(("seq", "ctx")),
            P(("seq", "ctx")),
            P(("seq", "ctx")),
            P(("seq", "ctx")),
            P(("seq", "ctx")),
            P(("seq", "ctx")),
        ),
        check_vma=False,
    )
```

profile of v0, /device:TPU:0, one launch (start us, length us, event | category | flops | bytes accessed | tf_op | source)
XLA Modules:
  0.0 593.7 jit_solution(3045953174442994015)
XLA Ops:
  16.3 42.2 %all-reduce.29 = (bf16[512]{0:T(512)(128)(2,1)S(1)}, bf16[512]{0:T(512)(128)(2,1)S(1)}, bf16[2048]{0:T(1024)(128)(2,1)S(1)}, bf16[512]{0:T(512)(128)(2,1)}, bf16...) all-reduce(bf16[512]{0:T(512)(128)(2,1)S(1)} %dynamic-update-slice., ...), channel_id=1, replica_groups=mesh['seq'=16,'ctx'=2] {'seq','ctx'}, use_global_device_ids=true, to_apply=%add.13 | all-reduce | flops 6656 | bytes 26624
  60.0 1.3 fusion.99
  61.3 7.3 %all-gather.8.cloned.1.call-done = bf16[786432]{0:T(1024)(128)(2,1)} async-done(((bf16[24576]{0:T(1024)(128)(2,1)}), bf16[786432]{0:T(1024)(128)(2,1)}) %all-gather.8.cloned.1.call-update) | async-done | bytes 1572880 | tf_op jit(solution)/shard_map/all_gather | solution.py:78
  68.6 3.3 reshape.478
  72.0 2.8 convolution_add_fusion
  74.7 3.5 copy.46
  78.3 1.8 slice_bitcast_fusion
  81.2 2.1 slice.70
  83.4 70.1 %all_gather.64 = bf16[262144]{0:T(1024)(128)(2,1)S(1)} all-gather(bf16[8192]{0:T(1024)(128)(2,1)S(1)} %copy-done.31), channel_id=1, replica_groups=mesh['seq'=16,'ctx'=2] {'seq','ctx'}, dimensions={0}, use_global_device_ids=true | all-gather | bytes 540672 | tf_op jit(solution)/shard_map/all_gather | solution.py:80
  153.8 1.3 convolution_convert_fusion
  156.3 2.1 slice_bitcast_fusion.2
  158.7 4.2 reshape.481
  162.9 13.5 %multiply_convert_fusion.6 = (bf16[512,2048]{1,0:T(8,128)(2,1)}, f32[512,2048]{1,0:T(8,128)}, f32[512,2048]{1,0:T(8,128)}) fusion(f32[2048]{0:T(1024)S(1)} %convert_element_type.166, bf16[512,2048]{1,0:T(8,128)(2,1)} %reshape.481, bf16[1,512,512]{2,1,0:T(8,128)(2,1)S(1)} %copy-done.4, f32[512]{0:T(512)S(1)} %convert_element_type.163, ...), kind=kOutput, calls=%fused_computation.85 | convolution fusion | flops 1144520704 | bytes 13123584 | tf_op jit(solution)/shard_map/dot_general | solution.py:170
  176.4 10.0 %all-gather.16.cloned.1.call-done = bf16[1048576]{0:T(1024)(128)(2,1)} async-done(((bf16[32768]{0:T(1024)(128)(2,1)}), bf16[1048576]{0:T(1024)(128)(2,1)}) %all-gather.16.cloned.1.call-update) | async-done | bytes 2097168 | tf_op jit(solution)/shard_map/all_gather | solution.py:84
  186.4 4.4 reshape.482
  190.8 6.4 %convert_reduce_fusion = (f32[2048]{0:T(1024)}, bf16[512,2048]{1,0:T(8,128)(2,1)S(1)}) fusion(f32[512,2048]{1,0:T(8,128)} %get-tuple-element.569, bf16[2048,512]{1,0:T(8,128)(2,1)} %reshape.482, bf16[1,512,512]{2,1,0:T(8,128)(2,1)S(1)} %copy-done.7, f32[512,2048]{1,0:T(8,128)} %get-tuple-element.614, f32[2048]{0:T(1024)S(1)} %convert_element_type.166), kind=kOutput, calls=%fused_computation.83 | convolution fusion | flops 1091565568 | bytes 13123584 | tf_op jit(solution)/shard_map/td,fd->tf/dot_general | solution.py:193
  197.1 1.3 copy-done.40
  198.4 1.4 convolution_bitcast_fusion.1
  199.9 3.0 copy.54
  202.8 1.3 convolution_bitcast_fusion
  204.1 3.0 copy.55
  207.2 1.4 all-gather.12.cloned.1.call-done
  208.6 4.6 while.59
  210.3 1.4 fusion.223
  211.7 1.5 fusion.224
  213.2 18.0 %all-gather.10.cloned.1.call-done = bf16[1024,512]{0,1:T(8,128)(2,1)} async-done(((bf16[512,512]{0,1:T(8,128)(2,1)}), bf16[1024,512]{0,1:T(8,128)(2,1)}) %all-gather.10.cloned.1.call-update) | async-done | bytes 1048592 | tf_op jit(solution)/shard_map/all_gather | solution.py:131
  231.2 5.6 while.61
  231.5 1.3 constant_dynamic-slice_fusion.16
  232.8 1.3 fusion.234
  234.1 2.8 fusion.235
  237.0 12.8 %while.62 = (s32[]{:T(128)}, f32[512,8,64]{0,2,1:T(8,128)S(1)}, s32[]{:T(128)}, bf16[1024,512]{0,1:T(8,128)(2,1)}, bf16[512,8,64]{0,2,1:T(8,128)(2,1)S(1)}, /*in...) while((s32[]{:T(128)}, f32[512,8,64]{0,2,1:T(8,128)S(1)}, ...), condition=%wide.region_12.13_spmd.clone, body=%wide.region_11.12_spmd.clone.sunk | while | flops 816317440 | bytes 24158400 | solution.py:228
  237.2 1.3 constant_dynamic-slice_fusion.17
  238.5 4.6 fusion.242
  243.1 6.7 %fusion.243 = f32[512,8,64]{0,2,1:T(8,128)S(1)} fusion(f32[512,8,64]{0,2,1:T(8,128)S(1)} %get-tuple-element.1102, bf16[512,8,64]{0,2,1:T(8,128)(2,1)S(1)} %bitcast.312, f32[8,512,512]{2,1,0:T(8,128)} %fusion.242, f32[8,512]{1,0:T(8,128)S(1)} %get-tuple-element.1123, f32[8,512]{1,0:T(8,128)S(1)} %get-tuple-element.1120, ...), kind=kOutput, calls=%fused_computation.51.clone.1 | convolution fusion | flops 547618816 | bytes 12353536 | tf_op jit(solution)/shard_map/while/body/hqk,khd->qhd/dot_general | solution.py:224
  249.8 22.0 %all_gather.75 = f32[1024,8]{0,1:T(8,128)S(1)} all-gather(f32[512,8]{0,1:T(8,128)S(1)} %bitcast.334), channel_id=1, replica_groups=mesh['seq'=16,'ctx'=2] {'ctx'}, dimensions={0}, use_global_device_ids=true | all-gather | bytes 49152 | tf_op jit(solution)/shard_map/all_gather | solution.py:237
  271.9 4.9 all_gather.73
  280.4 39.7 %while.63 = (s32[]{:T(128)}, f32[512,8,64]{0,2,1:T(8,128)}, f32[512,8,64]{0,2,1:T(8,128)}, bf16[1024,512]{0,1:T(8,128)(2,1)}, bf16[512,8,64]{0,2,1:T(8,128)(2,1)...) while((s32[]{:T(128)}, f32[512,8,64]{0,2,1:T(8,128)}, ...), condition=%wide.region_14.15_spmd.clone, body=%wide.region_13.0_spmd.clone.sunk | while | flops 1091306496 | bytes 35512512 | solution.py:273
  280.8 1.3 constant_dynamic-slice_fusion.18
  282.1 4.6 fusion.251
  286.6 7.8 %fusion.252 = f32[512,8,64]{0,2,1:T(8,128)} fusion(f32[512,8,64]{0,2,1:T(8,128)} %get-tuple-element.1060, bf16[512,8,64]{0,2,1:T(8,128)(2,1)S(1)} %bitcast.314, f32[8,512,512]{2,1,0:T(8,128)} %fusion.251, f32[8,512]{1,0:T(8,128)S(1)} %get-tuple-element.932, f32[8,512]{1,0:T(8,128)S(1)} %get-tuple-element.933, ...), kind=kOutput, calls=%fused_computation.71.clone.1 | convolution fusion | flops 547618816 | bytes 12353536 | tf_op jit(solution)/shard_map/while/body/hqk,qhd->khd/dot_general | solution.py:261
  294.5 5.8 fusion.253
  300.5 1.3 constant_dynamic-slice_fusion.18
  301.8 4.6 fusion.251
  306.4 7.8 %fusion.252 = f32[512,8,64]{0,2,1:T(8,128)} fusion(f32[512,8,64]{0,2,1:T(8,128)} %get-tuple-element.1060, bf16[512,8,64]{0,2,1:T(8,128)(2,1)S(1)} %bitcast.314, f32[8,512,512]{2,1,0:T(8,128)} %fusion.251, f32[8,512]{1,0:T(8,128)S(1)} %get-tuple-element.932, f32[8,512]{1,0:T(8,128)S(1)} %get-tuple-element.933, ...), kind=kOutput, calls=%fused_computation.71.clone.1 | convolution fusion | flops 547618816 | bytes 12353536 | tf_op jit(solution)/shard_map/while/body/hqk,qhd->khd/dot_general | solution.py:261
  314.2 5.8 fusion.253
  320.0 2.3 split.28
  322.3 1.9 slice_multiply_fusion.2
  325.3 5.8 while.60
  326.4 4.7 fusion.229
  331.1 1.4 convert_element_type.159
  332.5 1.4 convert_bitcast_fusion.1
  340.5 2.9 fusion.138
  343.5 4.5 reshape.487
  348.7 3.6 fusion.151
  352.4 2.2 convolution_add_fusion.2
  354.7 3.2 fusion.144
  358.9 1.5 convert_reduce_fusion.3
  360.5 41.0 %all-reduce.27 = (f32[512]{0:T(512)S(1)}, f32[512]{0:T(512)S(1)}, f32[512]{0:T(512)S(1)}, f32[512]{0:T(512)S(1)}, f32[1536]{0:T(1024)S(1)}, /*index=5*/f32[512]{0:T(512)S(1)}, f32[2048]{0:T(1024)S(1)}) all-reduce(f32[512]{0:T(512)S(1)} %get-tuple-element.458, ...), channel_id=2, replica_groups=mesh['seq'=16,'ctx'=2] {'seq','ctx'}, use_global_device_ids=true, to_apply=%region_20.21.clone | all-reduce | flops 6144 | bytes 49152
  405.0 2.5 fusion.92
  407.5 172.6 %all-reduce.32.cloned.1.call-done = (f32[786432]{0:T(1024)}, f32[262144]{0:T(1024)}, f32[1048576]{0:T(1024)}, f32[1048576]{0:T(1024)}) async-done(((f32[786432]{0:T(1024)}, f32[262144]{0:T(1024)}, f32[1048576]{0:T(1024)}, f32[1048576]{0:T(1024)}), (f32[786432]{0:T(1024)}, f32[262144]{0:T(1024)}, f32[1048576]{0:T(1024)}, f32[1048576]{0:T(1024)})) %all-reduce.32.cloned.1.call-update) | async-done | bytes 12582928
  580.1 1.6 dynamic-slice.8
  581.7 1.6 dynamic-slice.10
  583.2 1.5 dynamic-slice.4
  584.8 1.4 dynamic-slice.6
  (193 shorter events, 33.8 us)
Async XLA Ops:
  7.2 64.8 %copy-start.4 = (bf16[1,512,512]{2,1,0:T(8,128)(2,1)S(1)}, bf16[1,512,512]{2,1,0:T(8,128)(2,1)}, u32[]{:S(2)}) copy-start(bf16[1,512,512]{2,1,0:T(8,128)(2,1)} %param.24) | copy-start | bytes 1572868
  7.2 61.4 %all-gather.8.cloned.1.call-start = ((), (), s32[]{:S(2)}) async-start(), calls=%async_computation | async-start | bytes 1622016 | tf_op jit(solution)/shard_map/all_gather | solution.py:78
  7.9 150.8 %all-gather.14.cloned.1.call-start = ((), (), s32[]{:S(2)}) async-start(), calls=%async_computation.3 | async-start | bytes 2162688 | tf_op jit(solution)/shard_map/all_gather | solution.py:82
  8.7 177.7 %all-gather.16.cloned.1.call-start = ((), (), s32[]{:S(2)}) async-start(), calls=%async_computation.4 | async-start | bytes 2162688 | tf_op jit(solution)/shard_map/all_gather | solution.py:84
  9.4 199.1 %all-gather.12.cloned.1.call-start = ((), (), s32[]{:S(2)}) async-start(), calls=%async_computation.2 | async-start | bytes 1572864 | tf_op jit(solution)/shard_map/all_gather | solution.py:130
  58.5 16.2 %copy-start.23 = (f32[512]{0:T(512)}, f32[512]{0:T(512)S(1)}, u32[]{:S(2)}) copy-start(f32[512]{0:T(512)S(1)} %convert_element_type.147) | copy-start | bytes 6148
  58.5 16.2 %copy-start.33 = (f32[512]{0:T(512)}, f32[512]{0:T(512)S(1)}, u32[]{:S(2)}) copy-start(f32[512]{0:T(512)S(1)} %convert_element_type.148) | copy-start | bytes 6148
  58.7 96.6 %copy-start.17 = (f32[512,16]{0,1:T(8,128)}, f32[512,16]{0,1:T(8,128)S(1)}, u32[]{:S(2)}) copy-start(f32[512,16]{0,1:T(8,128)S(1)} %get-tuple-element.610) | copy-start | bytes 98308
  58.7 96.6 %copy-start.19 = (f32[512,16]{0,1:T(8,128)}, f32[512,16]{0,1:T(8,128)S(1)}, u32[]{:S(2)}) copy-start(f32[512,16]{0,1:T(8,128)S(1)} %get-tuple-element.611) | copy-start | bytes 98308
  59.9 137.2 %copy-start.21 = (f32[512]{0:T(512)}, f32[512]{0:T(512)S(1)}, u32[]{:S(2)}) copy-start(f32[512]{0:T(512)S(1)} %broadcast_multiply_fusion.2) | copy-start | bytes 6148
  61.3 13.4 %copy-start.29 = (f32[512]{0:T(512)}, f32[512]{0:T(512)S(1)}, u32[]{:S(2)}) copy-start(f32[512]{0:T(512)S(1)} %fusion.99) | copy-start | bytes 6148
  61.3 135.8 %copy-start.25 = (f32[512]{0:T(512)}, f32[512]{0:T(512)S(1)}, u32[]{:S(2)}) copy-start(f32[512]{0:T(512)S(1)} %fusion.137) | copy-start | bytes 6148
  71.9 2.8 copy-start.14
  78.3 5.1 copy-start.31
  80.1 73.7 %copy-start.7 = (bf16[1,512,512]{2,1,0:T(8,128)(2,1)S(1)}, bf16[1,512,512]{2,1,0:T(8,128)(2,1)}, u32[]{:S(2)}) copy-start(bf16[1,512,512]{2,1,0:T(8,128)(2,1)} %param.25) | copy-start | bytes 1572868
  81.1 150.1 %all-gather.10.cloned.1.call-start = ((), (), s32[]{:S(2)}) async-start(), calls=%async_computation.1 | async-start | bytes 1572864 | tf_op jit(solution)/shard_map/all_gather | solution.py:131
  83.3 194.5 %all-gather.20.cloned.1.call-start = ((), (), s32[]{:S(2)}) async-start(), calls=%async_computation.6 | async-start | bytes 1572864 | tf_op jit(solution)/shard_map/all_gather | solution.py:233
  153.8 9.1 %copy-start.9 = (bf16[512,512]{1,0:T(8,128)(2,1)}, bf16[512,512]{1,0:T(8,128)(2,1)S(1)}, u32[]{:S(2)}) copy-start(bf16[512,512]{1,0:T(8,128)(2,1)S(1)} %reshape.480) | copy-start | bytes 1572868
  155.1 123.0 %all-gather.18.cloned.1.call-start = ((), (), s32[]{:S(2)}) async-start(), calls=%async_computation.5 | async-start | bytes 1572864 | tf_op jit(solution)/shard_map/all_gather | solution.py:232
  155.2 41.9 %copy-start.27 = (f32[512]{0:T(512)}, f32[512]{0:T(512)S(1)}, u32[]{:S(2)}) copy-start(f32[512]{0:T(512)S(1)} %convert_element_type.162) | copy-start | bytes 6148
  158.4 421.7 %all-reduce.32.cloned.1.call-start = ((), (), s32[]{:S(2)}) async-start(), calls=%async_computation.7 | async-start | bytes 25165824
  197.1 1.3 copy-start.40
  199.9 3.0 copy-start.38
  204.1 4.4 copy-start
  208.5 22.7 %copy-start.12 = (bf16[512,512]{0,1:T(8,128)(2,1)S(1)}, bf16[512,512]{0,1:T(8,128)(2,1)}, u32[]{:S(2)}) copy-start(bf16[512,512]{0,1:T(8,128)(2,1)} %convolution_convert_fusion) | copy-start | bytes 1572868
  249.8 30.5 %copy-start.3 = (bf16[512,8,64]{0,2,1:T(8,128)(2,1)S(1)}, bf16[512,8,64]{0,2,1:T(8,128)(2,1)}, u32[]{:S(2)}) copy-start(bf16[512,8,64]{0,2,1:T(8,128)(2,1)} %maximum_convert_fusion) | copy-start | bytes 1572868
  249.8 30.5 %copy-start.16 = (bf16[512,8,64]{0,2,1:T(8,128)(2,1)S(1)}, bf16[512,8,64]{0,2,1:T(8,128)(2,1)}, u32[]{:S(2)}) copy-start(bf16[512,8,64]{0,2,1:T(8,128)(2,1)} %slice_bitcast_fusion.2) | copy-start | bytes 1572868
  280.4 41.9 %copy-start.20 = (f32[512,16]{0,1:T(8,128)S(1)}, f32[512,16]{0,1:T(8,128)}, u32[]{:S(2)}) copy-start(f32[512,16]{0,1:T(8,128)} %copy-done.19) | copy-start | bytes 98308
  320.0 5.3 copy-start.1
  320.0 5.3 copy-start.2
  331.1 4.9 copy-start.8
  331.1 6.6 %copy-start.6 = (f32[512,8,64]{0,2,1:T(8,128)S(1)}, f32[512,8,64]{0,2,1:T(8,128)}, u32[]{:S(2)}) copy-start(f32[512,8,64]{0,2,1:T(8,128)} %broadcast_multiply_fusion) | copy-start | bytes 3145732
  331.1 6.6 %copy-start.18 = (f32[512,16]{0,1:T(8,128)S(1)}, f32[512,16]{0,1:T(8,128)}, u32[]{:S(2)}) copy-start(f32[512,16]{0,1:T(8,128)} %copy-done.17) | copy-start | bytes 98308
  332.5 6.2 %copy-start.11 = (f32[512,8,48]{0,2,1:T(8,128)S(1)}, f32[512,8,48]{0,2,1:T(8,128)}, u32[]{:S(2)}) copy-start(f32[512,8,48]{0,2,1:T(8,128)} %split.28) | copy-start | bytes 2359300
  333.9 5.0 slice-start
  338.8 1.7 copy-start.5
  338.8 1.7 copy-start.22
  338.8 1.7 copy-start.24
  338.8 1.7 copy-start.26
  338.9 1.7 copy-start.34
  339.4 1.1 copy-start.15
  348.0 0.7 copy-start.36
  348.0 0.7 copy-start.35
  348.7 3.7 copy-start.13
  348.7 3.7 copy-start.39
  352.4 2.3 copy-start.28
  354.7 3.3 copy-start.30
  357.9 2.5 copy-start.32
  357.9 47.1 %copy-start.10 = (bf16[512,512]{1,0:T(8,128)(2,1)S(1)}, bf16[512,512]{1,0:T(8,128)(2,1)}, u32[]{:S(2)}) copy-start(bf16[512,512]{1,0:T(8,128)(2,1)} %copy-done.9) | copy-start | bytes 1572868
  402.1 184.6 %copy-start.37 = (f32[16]{0:T(128)}, f32[16]{0:T(128)S(1)}, u32[]{:S(2)}) copy-start(f32[16]{0:T(128)S(1)} %dynamic-slice.7) | copy-start | bytes 196
Sparse Core Ops, SparseCore 0:
  10.9 57.7 all-gather.7
  71.6 56.1 all-gather.13
  130.8 55.5 all-gather.15
  188.4 20.1 all-gather.11
  209.9 21.2 all-gather.9
  232.6 21.2 all-gather.19
  256.1 21.9 all-gather.17
  348.2 231.8 all-reduce.31
where the time goes:
time: 601 us; the launch traced here: 594 us
  waiting for transfers between devices  212 us (35%)
  blocking collectives  180 us (30%)
  matrix products  99.5 us (17%)
  local copies, waits for them, and re-layouts  66.8 us (11%)
  other arithmetic  19.2 us (3%)
  between operations  15 us (2%)
    unnamed x9, waiting for transfers between devices  175 us
    unnamed x2, blocking collectives  83.2 us
    all_gather x1, blocking collectives, body(): lax.all_gather(dense_weight, ('seq', 'ctx'), axis=0, tiled=True)  70.1 us
    unnamed x113, local copies, waits for them, and re-layouts  27.4 us
    all_gather x1, blocking collectives, body(): lax.all_gather(jnp.transpose(delta), 'ctx', axis=0, tiled=True)  22 us
    all_gather x1, waiting for transfers between devices, body(): lax.all_gather(value_own, 'ctx', axis=0, tiled=True)  18 us
    dot_general x2, matrix products, owner_step(): jnp.einsum('hqk,qhd->khd', grad_scores, queries, preferred_element_type=j...  15.7 us
    dot_general x1, matrix products, body(): jnp.dot(mlp_low, expand_weight, preferred_element_type=jnp.float32)  13.5 us
  transfers between devices with their start and end apart: 8, of which 6 were waited for; matrix products, arithmetic and copies ran while one was open for 18% of the time, Pallas kernels for 0%

commit v1 on v0

--- a/solution.py
+++ b/solution.py
@@ -1,6 +1,12 @@
+import functools
+import types
+
 import jax
 import jax.numpy as jnp
+import numpy as np
 from jax import lax
+from jax.experimental import pallas as pl
+from jax.experimental.pallas import tpu as pltpu
 from jax.sharding import PartitionSpec as P
 
 D = 512
@@ -9,6 +15,7 @@
 
 
 EPS = 1e-05
+BOTH = ("seq", "ctx")
 ROPE_BASE = 10000.0
 NEG = -1e30
 
@@ -71,18 +78,18 @@
         reduce_flat,
         reduce_bias,
     ) = (
-        lax.all_gather(attn_norm_gain, ("seq", "ctx"), axis=0, tiled=True),
-        lax.all_gather(attn_norm_bias, ("seq", "ctx"), axis=0, tiled=True),
-        lax.all_gather(mlp_norm_gain, ("seq", "ctx"), axis=0, tiled=True),
-        lax.all_gather(mlp_norm_bias, ("seq", "ctx"), axis=0, tiled=True),
-        lax.all_gather(qkv_weight, ("seq", "ctx"), axis=0, tiled=True),
-        lax.all_gather(qkv_bias, ("seq", "ctx"), axis=0, tiled=True),
-        lax.all_gather(dense_weight, ("seq", "ctx"), axis=0, tiled=True),
-        lax.all_gather(dense_bias, ("seq", "ctx"), axis=0, tiled=True),
-        lax.all_gather(fc_in_weight, ("seq", "ctx"), axis=0, tiled=True),
-        lax.all_gather(fc_in_bias, ("seq", "ctx"), axis=0, tiled=True),
-        lax.all_gather(fc_out_weight, ("seq", "ctx"), axis=0, tiled=True),
-        lax.all_gather(fc_out_bias, ("seq", "ctx"), axis=0, tiled=True),
+        lax.all_gather(attn_norm_gain, BOTH, axis=0, tiled=True),
+        lax.all_gather(attn_norm_bias, BOTH, axis=0, tiled=True),
+        lax.all_gather(mlp_norm_gain, BOTH, axis=0, tiled=True),
+        lax.all_gather(mlp_norm_bias, BOTH, axis=0, tiled=True),
+        lax.all_gather(qkv_weight, BOTH, axis=0, tiled=True),
+        lax.all_gather(qkv_bias, BOTH, axis=0, tiled=True),
+        lax.all_gather(dense_weight, BOTH, axis=0, tiled=True),
+        lax.all_gather(dense_bias, BOTH, axis=0, tiled=True),
+        lax.all_gather(fc_in_weight, BOTH, axis=0, tiled=True),
+        lax.all_gather(fc_in_bias, BOTH, axis=0, tiled=True),
+        lax.all_gather(fc_out_weight, BOTH, axis=0, tiled=True),
+        lax.all_gather(fc_out_bias, BOTH, axis=0, tiled=True),
     )
     mix_weight, proj_weight, expand_weight, reduce_weight = matrices(
         mix_flat, proj_flat, expand_flat, reduce_flat
@@ -177,10 +184,10 @@
     ) + reduce_bias.astype(jnp.float32)
     layer_out = (rows + branch_attn + branch_mlp).astype(jnp.bfloat16).reshape(shape)
     back_mix, back_proj, back_expand, back_reduce = (
-        lax.all_gather(qkv_weight, ("seq", "ctx"), axis=0, tiled=True),
-        lax.all_gather(dense_weight, ("seq", "ctx"), axis=0, tiled=True),
-        lax.all_gather(fc_in_weight, ("seq", "ctx"), axis=0, tiled=True),
-        lax.all_gather(fc_out_weight, ("seq", "ctx"), axis=0, tiled=True),
+        lax.all_gather(qkv_weight, BOTH, axis=0, tiled=True),
+        lax.all_gather(dense_weight, BOTH, axis=0, tiled=True),
+        lax.all_gather(fc_in_weight, BOTH, axis=0, tiled=True),
+        lax.all_gather(fc_out_weight, BOTH, axis=0, tiled=True),
     )
     back_mix, back_proj, back_expand, back_reduce = matrices(
         back_mix, back_proj, back_expand, back_reduce
@@ -283,20 +290,20 @@
     input_mlp, gain_mlp_grad, shift_mlp_grad = mlp_norm_back(grad_mlp_in)
     grad_tokens = (grad_float + input_attn + input_mlp).astype(jnp.bfloat16).reshape(shape)
     sums = (
-        lax.psum_scatter(gain_attn_grad, ("seq", "ctx"), scatter_dimension=0, tiled=True),
-        lax.psum_scatter(shift_attn_grad, ("seq", "ctx"), scatter_dimension=0, tiled=True),
-        lax.psum_scatter(gain_mlp_grad, ("seq", "ctx"), scatter_dimension=0, tiled=True),
-        lax.psum_scatter(shift_mlp_grad, ("seq", "ctx"), scatter_dimension=0, tiled=True),
-        lax.psum_scatter(grad_mix_w.reshape(-1), ("seq", "ctx"), scatter_dimension=0, tiled=True),
-        lax.psum_scatter(grad_mix_b, ("seq", "ctx"), scatter_dimension=0, tiled=True),
-        lax.psum_scatter(grad_proj.reshape(-1), ("seq", "ctx"), scatter_dimension=0, tiled=True),
-        lax.psum_scatter(grad_out_bias, ("seq", "ctx"), scatter_dimension=0, tiled=True),
+        lax.psum_scatter(gain_attn_grad, BOTH, scatter_dimension=0, tiled=True),
+        lax.psum_scatter(shift_attn_grad, BOTH, scatter_dimension=0, tiled=True),
+        lax.psum_scatter(gain_mlp_grad, BOTH, scatter_dimension=0, tiled=True),
+        lax.psum_scatter(shift_mlp_grad, BOTH, scatter_dimension=0, tiled=True),
+        lax.psum_scatter(grad_mix_w.reshape(-1), BOTH, scatter_dimension=0, tiled=True),
+        lax.psum_scatter(grad_mix_b, BOTH, scatter_dimension=0, tiled=True),
+        lax.psum_scatter(grad_proj.reshape(-1), BOTH, scatter_dimension=0, tiled=True),
+        lax.psum_scatter(grad_out_bias, BOTH, scatter_dimension=0, tiled=True),
         lax.psum_scatter(
-            grad_expand_w.reshape(-1), ("seq", "ctx"), scatter_dimension=0, tiled=True
+            grad_expand_w.reshape(-1), BOTH, scatter_dimension=0, tiled=True
         ),
-        lax.psum_scatter(grad_expand_b, ("seq", "ctx"), scatter_dimension=0, tiled=True),
-        lax.psum_scatter(grad_reduce.reshape(-1), ("seq", "ctx"), scatter_dimension=0, tiled=True),
-        lax.psum_scatter(grad_out_bias, ("seq", "ctx"), scatter_dimension=0, tiled=True),
+        lax.psum_scatter(grad_expand_b, BOTH, scatter_dimension=0, tiled=True),
+        lax.psum_scatter(grad_reduce.reshape(-1), BOTH, scatter_dimension=0, tiled=True),
+        lax.psum_scatter(grad_out_bias, BOTH, scatter_dimension=0, tiled=True),
     )
     return (
         layer_out,
@@ -316,41 +323,747 @@
     )
 
 
-def solution(mesh):
+def general(mesh):
     return jax.shard_map(
         body,
         mesh=mesh,
         in_specs=(
             P("seq", "ctx", None),
             P("seq", "ctx", None),
-            P(("seq", "ctx")),
-            P(("seq", "ctx")),
-            P(("seq", "ctx")),
-            P(("seq", "ctx")),
-            P(("seq", "ctx")),
-            P(("seq", "ctx")),
-            P(("seq", "ctx")),
-            P(("seq", "ctx")),
-            P(("seq", "ctx")),
-            P(("seq", "ctx")),
-            P(("seq", "ctx")),
-            P(("seq", "ctx")),
+            P(BOTH),
+            P(BOTH),
+            P(BOTH),
+            P(BOTH),
+            P(BOTH),
+            P(BOTH),
+            P(BOTH),
+            P(BOTH),
+            P(BOTH),
+            P(BOTH),
+            P(BOTH),
+            P(BOTH),
         ),
         out_specs=(
             P("seq", "ctx", None),
             P("seq", "ctx", None),
-            P(("seq", "ctx")),
-            P(("seq", "ctx")),
-            P(("seq", "ctx")),
-            P(("seq", "ctx")),
-            P(("seq", "ctx")),
-            P(("seq", "ctx")),
-            P(("seq", "ctx")),
-            P(("seq", "ctx")),
-            P(("seq", "ctx")),
-            P(("seq", "ctx")),
-            P(("seq", "ctx")),
-            P(("seq", "ctx")),
+            P(BOTH),
+            P(BOTH),
+            P(BOTH),
+            P(BOTH),
+            P(BOTH),
+            P(BOTH),
+            P(BOTH),
+            P(BOTH),
+            P(BOTH),
+            P(BOTH),
+            P(BOTH),
+            P(BOTH),
         ),
         check_vma=False,
     )
+
+
+MESH = pl.DeviceIdType.MESH
+F32, BF16 = jnp.float32, jnp.bfloat16
+HD = D // HEADS
+AX = "zycx"
+NN = (((1,), (0,)), ((), ()))
+NT = (((1,), (1,)), ((), ()))
+TN = (((0,), (0,)), ((), ()))
+QB = 256
+
+
+def mm(a, b, dims=NN):
+    return lax.dot_general(a, b, dims, preferred_element_type=F32)
+
+
+def iota(shape, dim):
+    return lax.broadcasted_iota(jnp.int32, shape, dim)
+
+
+def fused(sizes, names, *refs):
+    held = dict(zip(names, refs))
+    r = types.SimpleNamespace(**held)
+    X = sizes["x"]
+    C = sizes["c"]
+    Y = sizes["y"]
+    Z = sizes["z"]
+    N = Z * Y * C * X
+    T = r.tokens.shape[0]
+    S = T * X
+    HC = HEADS // X
+    HW = HC * HD
+    s = lax.axis_index("seq")
+    me = {"x": lax.axis_index("ctx"), "c": s % C, "y": (s // C) % Y, "z": s // (C * Y)}
+    x = me["x"]
+    xo = 1 - x
+
+    def device(at):
+        return ((at["z"] * Y + at["y"]) * C + at["c"], at["x"])
+
+    def others(axis):
+        n = sizes[axis]
+        return [dict(me, **{axis: (me[axis] + d) % n}) for d in range(1, n)]
+
+    flight = {}
+    count = [0]
+
+    def push(key, src, dst, at):
+        k = count[0]
+        count[0] += 1
+        cp = pltpu.make_async_remote_copy(
+            src_ref=src,
+            dst_ref=dst,
+            send_sem=r.send.at[k],
+            recv_sem=r.recv.at[k],
+            device_id=device(at),
+            device_id_type=MESH,
+        )
+        cp.start()
+        flight.setdefault(key, []).append(cp)
+
+    def wait(key):
+        for cp in flight.pop(key):
+            cp.wait()
+
+    def where_at(at, free):
+        return tuple(slice(None) if a in free else at[a] for a in AX)
+
+    def gather(name, axis, known):
+        ref = held[name]
+        part = ref.at[where_at(me, known)]
+        for at in others(axis):
+            push(name + axis, part, part, at)
+
+    def scatter(name, axis, done):
+        ref = held["g" + name]
+        free = [a for a in AX if a not in done and a != axis]
+        for k, at in enumerate(others(axis)):
+            push("g" + name + axis, ref.at[where_at(at, free)], held["r" + name + axis].at[k], at)
+
+    def add_parts(name, axis, done, finish=None):
+        wait("g" + name + axis)
+        ref, got = held["g" + name], held["r" + name + axis]
+        free = [a for a in AX if a not in done and a != axis]
+        total = 1
+        for a in free:
+            total *= sizes[a]
+
+        def one(i, _):
+            at, rest = dict(me), i
+            for a in reversed(free):
+                at[a] = rest % sizes[a]
+                rest = rest // sizes[a]
+            spot = tuple(at[a] for a in AX)
+            inner = tuple(at[a] for a in free)
+            acc = ref[spot].astype(F32)
+            for k in range(sizes[axis] - 1):
+                acc = acc + got[(k,) + inner].astype(F32)
+            if finish is None:
+                ref[spot] = acc.astype(ref.dtype)
+            else:
+                finish(acc)
+            return 0
+
+        if total == 1:
+            one(0, 0)
+        else:
+            lax.fori_loop(0, total, one, 0)
+
+    barrier = pltpu.get_barrier_semaphore()
+    greet = [at for a in AX for at in others(a)]
+    for at in greet:
+        pl.semaphore_signal(barrier, inc=1, device_id=device(at), device_id_type=MESH)
+
+    tmp = r.tmp
+    lane = iota((1, 128), 1)
+
+    def own(name):
+        return held[name].at[me["z"], me["y"], me["c"], x]
+
+    tmp[0 : r.fq.shape[0], :] = r.fq[...].astype(F32)
+    rows = r.fq.shape[0] * 128 // (3 * D)
+    per = 3 * D // 128
+
+    def block64(b, to_high):
+        v = tmp[pl.ds(b // 2, rows, stride=per), :]
+        return pltpu.roll(v, 64, 1) if (b % 2 == 1) != to_high else v
+
+    for half in range(X):
+        for jj in range(3):
+            for pair in range(HC // 2):
+                h0 = half * HC + 2 * pair
+                low = block64(3 * h0 + jj, False)
+                high = block64(3 * (h0 + 1) + jj, True)
+                at = jj * HW + pair * 128
+                r.sq[half, :, at : at + 128] = jnp.where(lane < 64, low, high).astype(BF16)
+
+    def reshard(src, name, width):
+        n = held[src].shape[0]
+        k = width // 128
+        tmp[0:n, :] = held[src][...].astype(F32)
+        dst = own(name)
+        for j in range(k):
+            dst[:, j * 128 : (j + 1) * 128] = tmp[pl.ds(j, n // k, stride=k), :].astype(BF16)
+
+    reshard("fd", "wd", D)
+    own("vec")[...] = r.vin[...]
+    own("wq")[...] = r.sq[x]
+
+    pl.semaphore_wait(barrier, len(greet))
+
+    at_x = others("x")[0]
+    push("wqx", r.sq.at[xo], own("wq"), at_x)
+    gather("vec", "x", "")
+    gather("wd", "x", "")
+    push("tok", r.tokens, r.tok2, at_x)
+    reshard("fi", "wi", FF)
+    reshard("fo", "wo", D)
+
+    rope = r.rope
+    mod = lane % HD
+
+    def rope_rows(i, _):
+        ch, sh = rope[0, pl.ds(i, 1), :], rope[1, pl.ds(i, 1), :]
+        cl, sl = rope[2], rope[3]
+        sine = sh * cl + ch * sl
+        at = pl.ds(pl.multiple_of(i * 32, 32), 32)
+        r.cos[at, :] = ch * cl - sh * sl
+        r.sinl[at, :] = jnp.where(mod < 8, -sine, 0.0)
+        r.sinh[at, :] = jnp.where(mod < 8, 0.0, sine)
+        return 0
+
+    def turn(u, at, sign):
+        return (
+            u * r.cos[at, :]
+            + sign * (pltpu.roll(u, 120, 1) * r.sinl[at, :] + pltpu.roll(u, 8, 1) * r.sinh[at, :])
+        )
+
+    wait("wqx")
+    gather("wq", "z", "x")
+    gather("wi", "z", "")
+    gather("wo", "z", "")
+    wait("vecx")
+    gather("vec", "y", "x")
+    wait("wdx")
+    gather("wd", "y", "x")
+
+    lax.fori_loop(0, S // 32, rope_rows, 0)
+
+    RC = 128
+
+    def norm_rows(src, base, keep):
+        def one(i, _):
+            v = src[pl.ds(pl.multiple_of(i * RC, RC), RC), :].astype(F32)
+            c = v - jnp.mean(v, axis=-1, keepdims=True)
+            scale = lax.rsqrt(jnp.mean(c * c, axis=-1, keepdims=True) + EPS)
+            r.n[pl.ds(pl.multiple_of(base + i * RC, RC), RC), :] = c * scale
+            if keep:
+                r.scale[pl.ds(pl.multiple_of(i * RC, RC), RC), :] = jnp.broadcast_to(scale, (RC, 128))
+            return 0
+
+        lax.fori_loop(0, T // RC, one, 0)
+
+    norm_rows(r.tokens, x * T, True)
+
+    wait("wqz")
+    gather("wq", "y", "xz")
+    wait("vecy")
+    gather("vec", "z", "xy")
+    wait("wdy")
+    gather("wd", "z", "xy")
+    wait("wiz")
+    gather("wi", "x", "z")
+    wait("vecz")
+    gather("vec", "c", "xyz")
+    wait("wdz")
+    gather("wd", "c", "xyz")
+    wait("wqy")
+    gather("wq", "c", "xyz")
+    wait("woz")
+    gather("wo", "x", "z")
+    wait("vecc")
+
+    widths = [D // N, D // N, D // N, D // N, 3 * D // N, D // N, FF // N, D // N]
+
+    def column(v, n):
+        j = iota((1, n), 1)
+        if v != 4:
+            return j
+        hh = (j % HW) // HD
+        return (x * HC + hh) * (3 * HD) + (j // HW) * HD + j % HD
+
+    def lengths(v):
+        return 3 * HW if v == 4 else widths[v] * N
+
+    vec2 = r.vec.reshape(N * 8, 128)
+
+    def expand(v):
+        n = lengths(v)
+        j = column(v, n)
+        pick = (iota((128, n), 0) == j % widths[v]).astype(F32).astype(BF16)
+        rows_v = vec2[pl.ds(v, N, stride=8), :].astype(BF16)
+        spread = mm(rows_v, pick)
+        r.vrow[v : v + 1, 0:n] = jnp.sum(
+            jnp.where(iota((N, n), 0) == j // widths[v], spread, 0.0), axis=0, keepdims=True
+        )
+
+    for v in range(8):
+        expand(v)
+
+    def row(v, n=D, off=0):
+        return r.vrow[v : v + 1, off : off + n]
+
+    def affine_attn(base):
+        def one(i, _):
+            at = pl.ds(pl.multiple_of(base + i * RC, RC), RC)
+            r.ha[at, :] = (r.n[at, :] * row(0) + row(1)).astype(BF16)
+            return 0
+
+        lax.fori_loop(0, T // RC, one, 0)
+
+    affine_attn(x * T)
+
+    def affine_mlp(i, _):
+        at = pl.ds(pl.multiple_of(x * T + i * RC, RC), RC)
+        to = pl.ds(pl.multiple_of(i * RC, RC), RC)
+        r.hm[to, :] = (r.n[at, :] * row(2) + row(3)).astype(BF16)
+        return 0
+
+    lax.fori_loop(0, T // RC, affine_mlp, 0)
+
+    wait("wdc")
+    wd = r.wd.reshape(D, D)
+    for k in range(D // QB):
+        r.do1[:, k * QB : (k + 1) * QB] = mm(
+            r.cot[...], wd[k * QB : (k + 1) * QB, :], NT
+        ).astype(BF16)
+    mine = pl.ds(pl.multiple_of(x * HW, HW), HW)
+    theirs = pl.ds(pl.multiple_of(xo * HW, HW), HW)
+    rows_mine = pl.ds(pl.multiple_of(x * T, T), T)
+    rows_theirs = pl.ds(pl.multiple_of(xo * T, T), T)
+    push("do", r.do1.at[:, theirs], r.do2.at[rows_mine, :], at_x)
+    r.do2[rows_mine, :] = r.do1[:, mine]
+
+    wait("wix")
+    gather("wi", "y", "zx")
+    wait("wox")
+    gather("wo", "y", "zx")
+
+    wait("tok")
+    norm_rows(r.tok2, xo * T, False)
+    affine_attn(xo * T)
+
+    wait("wqc")
+    wq = r.wq.reshape(D, 3 * HW)
+
+    def qkv_rows(i, _):
+        at = pl.ds(pl.multiple_of(i * QB, QB), QB)
+        h = r.ha[at, :]
+        for jj, name in enumerate("qkv"):
+            u = mm(h, wq[:, jj * HW : (jj + 1) * HW]) + row(4, HW, jj * HW)
+            for b in range(HW // 128):
+                w = u[:, b * 128 : (b + 1) * 128]
+                if jj < 2:
+                    w = turn(w, at, 1.0)
+                if jj == 0:
+                    w = w * HD**-0.5
+                w = w.astype(BF16)
+                held[name][at, b * 128 : (b + 1) * 128] = w
+                if jj >= 1:
+                    held[name + "t"][b * 128 : (b + 1) * 128, at] = w.T
+        return 0
+
+    lax.fori_loop(0, S // QB, qkv_rows, 0)
+
+    wait("wiy")
+    gather("wi", "c", "zxy")
+    wait("do")
+
+    r.dk[...] = jnp.zeros_like(r.dk)
+    r.dv[...] = jnp.zeros_like(r.dv)
+    causal = iota((QB, QB), 0) <= iota((QB, QB), 1)
+
+    def head(h, _):
+        lanes = pl.ds(pl.multiple_of((h // 2) * 128, 128), 128)
+        ours = (lane // HD) == h % 2
+        head_rows = pl.ds(pl.multiple_of(h * HD, HD), HD)
+        for i in range(S // QB):
+            here = slice(i * QB, (i + 1) * QB)
+            qm = jnp.where(ours, r.q[here, lanes], jnp.zeros((), BF16))
+            dom = jnp.where(ours, r.do2[here, lanes], jnp.zeros((), BF16))
+            top = None
+            for j in range(i + 1):
+                st = mm(r.k[j * QB : (j + 1) * QB, lanes], qm, NT)
+                if j == i:
+                    st = jnp.where(causal, st, NEG)
+                r.st[j] = st
+                part = jnp.max(st, axis=0, keepdims=True)
+                top = part if top is None else jnp.maximum(top, part)
+            total = None
+            for j in range(i + 1):
+                e = jnp.exp(r.st[j] - top)
+                r.st[j] = e
+                part = jnp.sum(e, axis=0, keepdims=True)
+                total = part if total is None else total + part
+            scale = 1.0 / total
+            delta = None
+            for j in range(i + 1):
+                p = r.st[j] * scale
+                r.st[j] = p
+                r.pb[j * QB : (j + 1) * QB, :] = p.astype(BF16)
+                dp = mm(r.v[j * QB : (j + 1) * QB, lanes], dom, NT)
+                r.dp[j] = dp
+                part = jnp.sum(p * dp, axis=0, keepdims=True)
+                delta = part if delta is None else delta + part
+            for j in range(i + 1):
+                ds = r.st[j] * (r.dp[j] - delta)
+                r.ds[j * QB : (j + 1) * QB, :] = ds.astype(BF16)
+            n = (i + 1) * QB
+            pb, ds = r.pb[0:n, :], r.ds[0:n, :]
+            r.ot[head_rows, here] = mm(r.vt[head_rows, 0:n], pb).astype(BF16)
+            r.dqt[head_rows, here] = mm(r.kt[head_rows, 0:n], ds)
+            r.dk[0:n, lanes] += mm(ds, qm)
+            r.dv[0:n, lanes] += mm(pb, dom)
+        return 0
+
+    lax.fori_loop(0, HC, head, 0)
+
+    push("o", r.ot.at[:, rows_theirs], r.of.at[mine, :], at_x)
+    r.of[mine, :] = r.ot[:, rows_mine]
+    wait("woy")
+    gather("wo", "c", "zxy")
+
+    r.vg[...] = jnp.zeros_like(r.vg)
+
+    def dqkv_rows(i, _):
+        at = pl.ds(pl.multiple_of(i * QB, QB), QB)
+        for b in range(HW // 128):
+            cols = slice(b * 128, (b + 1) * 128)
+            dq = r.dqt[cols, at].T
+            out = (
+                turn(dq, at, -1.0) * HD**-0.5,
+                turn(r.dk[at, cols], at, -1.0),
+                r.dv[at, cols],
+            )
+            for jj in range(3):
+                w = out[jj].astype(BF16)
+                to = slice(jj * HW + b * 128, jj * HW + (b + 1) * 128)
+                r.dqkv[at, to] = w
+                r.vg[4:5, to] += jnp.sum(w.astype(F32), axis=0, keepdims=True)
+        return 0
+
+    lax.fori_loop(0, S // QB, dqkv_rows, 0)
+
+    gq = r.gq.reshape(D, 3 * HW)
+    for k in range(D // QB):
+        gq[k * QB : (k + 1) * QB, :] = mm(
+            r.ha[:, k * QB : (k + 1) * QB], r.dqkv[...], TN
+        ).astype(BF16)
+    scatter("q", "c", "")
+
+    def dh_rows(base, mine_too):
+        def one(i, _):
+            at = pl.ds(pl.multiple_of(base + i * QB, QB), QB)
+            to = pl.ds(pl.multiple_of(i * QB, QB), QB)
+            dh = mm(r.dqkv[at, :], wq[...], NT)
+            r.vg[0:1, 0:D] += jnp.sum(dh * r.n[at, :], axis=0, keepdims=True)
+            r.vg[1:2, 0:D] += jnp.sum(dh, axis=0, keepdims=True)
+            u = dh * row(0)
+            if mine_too:
+                r.u[to, :] = u
+            else:
+                r.us[to, :] = u.astype(BF16)
+            return 0
+
+        lax.fori_loop(0, T // QB, one, 0)
+
+    dh_rows(xo * T, False)
+    push("u", r.us, r.ur, at_x)
+    add_parts("q", "c", "")
+    scatter("q", "y", "c")
+    dh_rows(x * T, True)
+
+    wait("wic")
+    wait("woc")
+    wi = r.wi.reshape(D, FF)
+    wo = r.wo.reshape(FF, D)
+    gi = r.gi.reshape(D, FF)
+    go = r.go.reshape(FF, D)
+    r.hmt[...] = r.hm[...].T
+    r.mo[...] = jnp.zeros_like(r.mo)
+    r.dm[...] = jnp.zeros_like(r.dm)
+    FB = 512
+
+    def ff_block(b, _):
+        cols = pl.ds(pl.multiple_of(b * FB, FB), FB)
+        f = mm(r.hm[...], wi[:, cols]) + r.vrow[6:7, cols]
+        phi = 0.5 + 0.5 * lax.erf(f * (0.5**0.5))
+        a = (f * phi).astype(BF16)
+        slope = phi + f * (jnp.exp(-0.5 * f * f) * (0.5 / np.pi) ** 0.5)
+        df = (mm(r.cot[...], wo[cols, :], NT) * slope).astype(BF16)
+        r.vg[6:7, cols] = jnp.sum(df.astype(F32), axis=0, keepdims=True)
+        r.mo[...] += mm(a, wo[cols, :])
+        r.dm[...] += mm(df, wi[:, cols], NT)
+        go[cols, :] = mm(a, r.cot[...], TN).astype(BF16)
+        gi[:, cols] = mm(r.hmt[...], df).astype(BF16)
+        return 0
+
+    lax.fori_loop(0, FF // FB, ff_block, 0)
+    scatter("i", "c", "")
+    scatter("o", "c", "")
+    add_parts("q", "y", "c")
+    scatter("q", "z", "cy")
+
+    wait("o")
+    r.gd.reshape(D, D)[...] = mm(r.of[...], r.cot[...]).astype(BF16)
+    scatter("d", "c", "")
+    g_sum = jnp.sum(r.cot[...].astype(F32), axis=0, keepdims=True)
+    r.vg[5:6, 0:D] = g_sum
+    r.vg[7:8, 0:D] = g_sum
+    own_n = r.n[rows_mine, :]
+    r.vg[2:3, 0:D] = jnp.sum(r.dm[...] * own_n, axis=0, keepdims=True)
+    r.vg[3:4, 0:D] = jnp.sum(r.dm[...], axis=0, keepdims=True)
+
+    gv2 = r.gv.reshape(N * 8, 128)
+
+    def collapse(v):
+        n = lengths(v)
+        j = column(v, n)
+        pick = (iota((128, n), 0) == j % widths[v]).astype(F32).astype(BF16)
+        left = jnp.where(iota((N, n), 0) == j // widths[v], r.vg[v : v + 1, 0:n], 0.0)
+        acc = None
+        for _ in range(3):
+            low = left.astype(BF16)
+            part = mm(low, pick, NT)
+            acc = part if acc is None else acc + part
+            left = left - low.astype(F32)
+        gv2[pl.ds(v, N, stride=8), :] = acc
+
+    for v in range(8):
+        collapse(v)
+    scatter("v", "c", "")
+
+    add_parts("i", "c", "")
+    scatter("i", "y", "c")
+    add_parts("o", "c", "")
+    scatter("o", "y", "c")
+    add_parts("d", "c", "")
+    scatter("d", "z", "c")
+    add_parts("v", "c", "")
+    scatter("v", "z", "c")
+
+    r.out[...] = (
+        r.tokens[...].astype(F32)
+        + mm(r.of[...], wd[...], TN)
+        + row(5)
+        + (r.mo[...] + row(7))
+    ).astype(BF16)
+
+    add_parts("q", "z", "cy")
+    wait_q = r.gq.at[me["z"], me["y"], me["c"], xo]
+    push("gqx", wait_q, r.rqx, at_x)
+
+    wait("u")
+
+    def final_rows(i, _):
+        at = pl.ds(pl.multiple_of(i * RC, RC), RC)
+        far = pl.ds(pl.multiple_of(x * T + i * RC, RC), RC)
+        u = r.u[at, :] + r.ur[at, :].astype(F32) + r.dm[at, :] * row(2)
+        n = r.n[far, :]
+        back = u - jnp.mean(u, axis=-1, keepdims=True) - n * jnp.mean(u * n, axis=-1, keepdims=True)
+        r.gtok[at, :] = (r.cot[at, :].astype(F32) + back * r.scale[at, 0:1]).astype(BF16)
+        return 0
+
+    lax.fori_loop(0, T // RC, final_rows, 0)
+
+    add_parts("i", "y", "c")
+    scatter("i", "x", "cy")
+    add_parts("o", "y", "c")
+    scatter("o", "x", "cy")
+    add_parts("d", "z", "c")
+    scatter("d", "y", "cz")
+    add_parts("v", "z", "c")
+    scatter("v", "y", "cz")
+    add_parts("d", "y", "cz")
+    scatter("d", "x", "czy")
+    add_parts("v", "y", "cz")
+    scatter("v", "x", "czy")
+    add_parts("i", "x", "cy")
+    scatter("i", "z", "cyx")
+    add_parts("o", "x", "cy")
+    scatter("o", "z", "cyx")
+
+    def flat(name, width):
+        out = held[name]
+        k = width // 128
+        n = out.shape[0] // k
+
+        def put(acc):
+            for j in range(k):
+                out[pl.ds(j, n, stride=k), :] = acc[:, j * 128 : (j + 1) * 128]
+
+        return put
+
+    wait("gqx")
+    half_own = r.gq[me["z"], me["y"], me["c"], x].astype(F32)
+    half_got = r.rqx[...].astype(F32)
+    lo_half = jnp.where(x == 0, half_own, half_got)
+    hi_half = jnp.where(x == 0, half_got, half_own)
+    halves = (lo_half, hi_half)
+
+    def piece(b, to_high):
+        h, jj = b // 3, b % 3
+        half, hh = h // HC, h % HC
+        at = jj * HW + (hh // 2) * 128
+        v = halves[half][:, at : at + 128]
+        return pltpu.roll(v, 64, 1) if (hh % 2 == 1) != to_high else v
+
+    for j in range(per):
+        both = jnp.where(lane < 64, piece(2 * j, False), piece(2 * j + 1, True))
+        r.oq[pl.ds(j, rows, stride=per), :] = both
+
+    def put_vec(acc):
+        r.ov[...] = acc
+
+    add_parts("d", "x", "czy", flat("od", D))
+    add_parts("v", "x", "czy", put_vec)
+    add_parts("i", "z", "cyx", flat("oi", FF))
+    add_parts("o", "z", "cyx", flat("oo", D))
+
+
+def rope_table(length):
+    lanes = np.arange(128) % HD
+    rot = HD // 4
+    inverse = np.where(lanes < rot, 1.0 / ROPE_BASE ** (2.0 * (lanes % (rot // 2)) / rot), 0.0)
+    high = 32.0 * np.arange(length // 32)[:, None] * inverse
+    low = np.arange(32)[:, None] * inverse
+    return np.stack([np.cos(high), np.sin(high), np.cos(low), np.sin(low)]).astype(np.float32)
+
+
+def layer(sizes, tokens, cotangent, *params):
+    Z, Y, C, X = (sizes[a] for a in AX)
+    N = Z * Y * C * X
+    T = tokens.shape[1]
+    S = T * X
+    HW = HEADS // X * HD
+    vectors = [params[i] for i in (0, 1, 2, 3, 5, 7, 9, 11)]
+    weights = [params[i] for i in (4, 6, 8, 10)]
+    vin = jnp.stack([jnp.pad(v.astype(F32), (0, 128 - v.shape[0])) for v in vectors])
+    flats = [w.reshape(-1, 128) for w in weights]
+    full = dict(z=Z, y=Y, c=C, x=X)
+
+    def parts(axis, done, slab, dtype, last=False):
+        free = [full[a] for a in AX if a not in done and a != axis]
+        return pltpu.VMEM((full[axis] - 1, *free, *slab), dtype)
+
+    slabs = {
+        "q": (D // N, 3 * HW),
+        "d": (D // N, D),
+        "i": (D // N, FF),
+        "o": (FF // N, D),
+        "v": (8, 128),
+    }
+    orders = {"q": "cyz", "d": "czyx", "i": "cyxz", "o": "cyxz", "v": "czyx"}
+    keep = types.SimpleNamespace()
+    scratch = vars(keep)
+    for k, slab in slabs.items():
+        kind = F32 if k == "v" else BF16
+        scratch["vec" if k == "v" else "w" + k] = pltpu.VMEM((Z, Y, C, X, *slab), kind)
+        scratch["g" + k] = pltpu.VMEM((Z, Y, C, X, *slab), kind)
+        for n, axis in enumerate(orders[k]):
+            scratch["r" + k + axis] = parts(axis, orders[k][:n], slab, kind)
+    keep.rqx = pltpu.VMEM(slabs["q"], BF16)
+    keep.sq = pltpu.VMEM((X, *slabs["q"]), BF16)
+    keep.tmp = pltpu.VMEM((max(f.shape[0] for f in flats), 128), F32)
+    keep.cos = keep.sinl = keep.sinh = pltpu.VMEM((S, 128), F32)
+    keep.tok2 = pltpu.VMEM((T, D), BF16)
+    keep.n = pltpu.VMEM((S, D), F32)
+    keep.scale = pltpu.VMEM((T, 128), F32)
+    keep.vrow = pltpu.VMEM((8, FF), F32)
+    keep.vg = pltpu.VMEM((8, FF), F32)
+    keep.ha = pltpu.VMEM((S, D), BF16)
+    keep.hm = pltpu.VMEM((T, D), BF16)
+    keep.hmt = pltpu.VMEM((D, T), BF16)
+    keep.do1 = pltpu.VMEM((T, D), BF16)
+    keep.q = keep.k = keep.v = keep.do2 = pltpu.VMEM((S, HW), BF16)
+    keep.kt = keep.vt = keep.ot = pltpu.VMEM((HW, S), BF16)
+    keep.dqt = pltpu.VMEM((HW, S), F32)
+    keep.dk = pltpu.VMEM((S, HW), F32)
+    keep.dv = pltpu.VMEM((S, HW), F32)
+    keep.st = pltpu.VMEM((S // QB, QB, QB), F32)
+    keep.dp = pltpu.VMEM((S // QB, QB, QB), F32)
+    keep.pb = pltpu.VMEM((S, QB), BF16)
+    keep.ds = pltpu.VMEM((S, QB), BF16)
+    keep.dqkv = pltpu.VMEM((S, 3 * HW), BF16)
+    keep.of = pltpu.VMEM((D, T), BF16)
+    keep.u = pltpu.VMEM((T, D), F32)
+    keep.us = pltpu.VMEM((T, D), BF16)
+    keep.ur = pltpu.VMEM((T, D), BF16)
+    keep.mo = pltpu.VMEM((T, D), F32)
+    keep.dm = pltpu.VMEM((T, D), F32)
+    copies = 4 * (2 * (Z - 1) + 2 * 3) + 2 * (Z + 2) + 16
+    keep.send = pltpu.SemaphoreType.DMA((copies,))
+    keep.recv = pltpu.SemaphoreType.DMA((copies,))
+    ins = "tokens cot fq fd".split() + "fi fo vin rope".split()
+    outs = dict(
+        out=jax.ShapeDtypeStruct((T, D), BF16),
+        gtok=jax.ShapeDtypeStruct((T, D), BF16),
+        oq=jax.ShapeDtypeStruct(flats[0].shape, F32),
+        od=jax.ShapeDtypeStruct(flats[1].shape, F32),
+        oi=jax.ShapeDtypeStruct(flats[2].shape, F32),
+        oo=jax.ShapeDtypeStruct(flats[3].shape, F32),
+        ov=jax.ShapeDtypeStruct((8, 128), F32),
+    )
+    vmem = pl.BlockSpec(memory_space=pltpu.VMEM)
+    names = ins + list(outs) + list(scratch)
+    out, gtok, gq, gd, gi, go, gv = pl.pallas_call(
+        functools.partial(fused, sizes, names),
+        out_shape=list(outs.values()),
+        in_specs=[vmem] * len(ins),
+        out_specs=[vmem] * len(outs),
+        scratch_shapes=list(scratch.values()),
+        compiler_params=pltpu.CompilerParams(
+            collective_id=0, has_side_effects=True, vmem_limit_bytes=67043328
+        ),
+        name="layer",
+    )(
+        tokens.reshape(T, D),
+        cotangent.reshape(T, D),
+        *flats,
+        vin,
+        jnp.asarray(rope_table(S)),
+    )
+    v = [gv[i, : p.shape[0]] for i, p in enumerate(vectors)]
+    return (
+        out.reshape(tokens.shape),
+        gtok.reshape(tokens.shape),
+        v[0],
+        v[1],
+        v[2],
+        v[3],
+        gq.reshape(-1),
+        v[4],
+        gd.reshape(-1),
+        v[5],
+        gi.reshape(-1),
+        v[6],
+        go.reshape(-1),
+        v[7],
+    )
+
+
+def solution(mesh):
+    n_seq, n_ctx = mesh.shape["seq"], mesh.shape["ctx"]
+    if n_ctx != 2 or n_seq % 4 or (D // (n_seq * n_ctx)) % 16:
+        return general(mesh)
+    sizes = {"z": n_seq // 4, "y": 2, "c": 2, "x": n_ctx}
+    flat = P(("seq", "ctx"))
+    rows = P("seq", "ctx", None)
+    return jax.shard_map(
+        functools.partial(layer, sizes),
+        mesh=mesh,
+        in_specs=(rows, rows) + (flat,) * 12,
+        out_specs=(rows, rows) + (flat,) * 12,
+        check_vma=False,
+    )

time: 601 us -> 132 us (0.22); the launches traced: 594 us -> 132 us
  waiting for transfers between devices: 212 us -> 0 us
  blocking collectives: 180 us -> 0 us
  Pallas kernels: 0 us -> 120 us
  matrix products: 99.5 us -> 0 us
  local copies, waits for them, and re-layouts: 66.8 us -> 10.8 us
  other arithmetic: 19.2 us -> 0.6 us
  between operations: 15 us -> 0.72 us
    unnamed x9 -> x0, waiting for transfers between devices: 175 us -> none
    pallas_call x0 -> x1, Pallas kernels: none -> 120 us  [layer(): pl.pallas_call(functools.partial(fused, sizes, names), out_shape=list(out...]
    dot_general x24 -> x0, matrix products: 99.5 us -> none  [the longest x2 15.7 us: owner_step(): jnp.einsum('hqk,qhd->khd', grad_scores, queries, preferred_element_type=j...]
    all_gather x3 -> x0, blocking collectives: 97 us -> none  [the longest x1 70.1 us: body(): lax.all_gather(dense_weight, ('seq', 'ctx'), axis=0, tiled=True)]
    unnamed x2 -> x0, blocking collectives: 83.2 us -> none
    all_gather x7 -> x0, waiting for transfers between devices: 37 us -> none  [the longest x1 18 us: body(): lax.all_gather(value_own, 'ctx', axis=0, tiled=True)]
    unnamed x113 -> x34, local copies, waits for them, and re-layouts: 27.4 us -> 9.2 us
    reshape x5 -> x0, local copies, waits for them, and re-layouts: 16.7 us -> none  [the longest x1 4.53 us: body(): grad_mix_w.reshape(-1)]
  transfers between devices with their start and end apart: 8 -> 0, of which waited for: 6 -> 0; matrix products, arithmetic and copies ran while one was open for 18% -> 0% of each run, Pallas kernels for 0% -> 0%
where the time goes in v1:
time: 132 us
  Pallas kernels  120 us (91%)
  local copies, waits for them, and re-layouts  10.8 us (8%)
    pallas_call x1, Pallas kernels, layer(): pl.pallas_call(functools.partial(fused, sizes, names), out_shape=list(out...  120 us
    unnamed x34, local copies, waits for them, and re-layouts  9.2 us

profile of v1, /device:TPU:0, one launch (start us, length us, event | category | flops | bytes accessed | tf_op | source)
XLA Modules:
  0.0 131.8 jit_solution(1727559054232190786)
XLA Ops:
  0.6 0.0 copy-start.6
  0.7 0.0 copy-start.7
  0.7 0.6 copy-done.6
  1.3 0.0 copy-done.7
  1.3 0.0 copy-start.8
  1.3 0.0 copy-start.9
  1.3 0.6 copy-done.8
  2.0 0.0 copy-done.9
  2.0 0.0 copy-start.10
  2.0 0.0 copy-start.11
  2.0 0.6 copy-done.10
  2.7 0.0 copy-done.11
  2.7 0.0 copy-start.12
  2.7 0.0 copy-start.13
  2.7 0.6 copy-done.12
  3.3 0.0 copy-done.13
  3.4 0.6 stack.46.refs_6_
  4.0 119.7 %layer.1 = (bf16[512,512]{1,0:T(8,128)(2,1)}, bf16[512,512]{1,0:T(8,128)(2,1)}, f32[192,128]{1,0:T(8,128)}, f32[64,128]{1,0:T(8,128)}, f32[256,128]{1,0:T(8,128)}, /*index=5*/f32[256,128]{1,0:T(8,128)}, f32[8,128]{1,0:T(8,128)}) custom-call(bf16[512,512]{1,0:T(8,128)(2,1)} %bitcast.44, bf16[512,512]{1,0:T(8,128)(2,1)} %bitcast.45, ...), custom_call_target="tpu_custom_call" | custom-call | tf_op jit(solution)/shard_map/layer/pallas_call | solution.py:1020
  123.7 0.0 copy-start.5
  123.7 0.7 copy-done.5
  124.4 0.5 slice_bitcast_fusion.3
  124.9 0.5 slice_bitcast_fusion.1
  125.4 0.5 slice_bitcast_fusion
  125.9 0.0 copy-start
  125.9 1.9 %copy.35 = bf16[1,512,512]{2,1,0:T(8,128)(2,1)} copy(bf16[1,512,512]{2,1,0:T(8,128)(2,1)} %bitcast.47) | data formatting | bytes 1048576
  127.8 0.0 copy-done
  127.9 0.0 copy-start.3
  127.9 0.8 copy.36
  128.6 0.2 copy-done.3
  128.8 0.0 copy-start.4
  128.8 0.0 copy-start.2
  128.8 0.6 copy.37
  129.5 0.1 copy-done.4
  129.6 0.6 copy.38
  130.2 0.0 copy-done.2
  130.2 0.0 copy-start.1
  130.2 0.7 copy.39
  130.9 0.3 copy-done.1
  131.1 0.7 copy.40
  (5 shorter events, 0.1 us)
Async XLA Ops:
  0.6 0.7 copy-start.6
  0.7 0.7 copy-start.7
  1.3 0.7 copy-start.8
  1.3 0.7 copy-start.9
  2.0 0.7 copy-start.10
  2.0 0.7 copy-start.11
  2.7 0.7 copy-start.12
  2.7 0.7 copy-start.13
  123.7 0.7 copy-start.5
  125.9 1.9 %copy-start = (bf16[512,512]{1,0:T(8,128)(2,1)S(1)}, bf16[512,512]{1,0:T(8,128)(2,1)}, u32[]{:S(2)}) copy-start(bf16[512,512]{1,0:T(8,128)(2,1)} %get-tuple-element.22) | copy-start | bytes 1572868
  127.9 1.0 copy-start.3
  128.8 0.8 copy-start.4
  128.8 1.4 %copy-start.2 = (f32[256,128]{1,0:T(8,128)S(1)}, f32[256,128]{1,0:T(8,128)}, u32[]{:S(2)}) copy-start(f32[256,128]{1,0:T(8,128)} %get-tuple-element.26) | copy-start | bytes 393220
  130.2 1.0 copy-start.1

commit v2 on v1

--- a/solution.py
+++ b/solution.py
@@ -393,6 +393,8 @@
     S = T * X
     HC = HEADS // X
     HW = HC * HD
+    FH = FF // X
+    CH = dict(q=384, i=FH // 2, o=D // 2)
     s = lax.axis_index("seq")
     me = {"x": lax.axis_index("ctx"), "c": s % C, "y": (s // C) % Y, "z": s // (C * Y)}
     x = me["x"]
@@ -426,25 +428,43 @@
         for cp in flight.pop(key):
             cp.wait()
 
-    def where_at(at, free):
-        return tuple(slice(None) if a in free else at[a] for a in AX)
-
-    def gather(name, axis, known):
-        ref = held[name]
-        part = ref.at[where_at(me, known)]
+    def axes(name):
+        return AX[: 3 if name == "o" else 4]
+
+    def chunk(name, k):
+        if k is None:
+            return slice(None)
+        w = CH[name]
+        return slice(k * w, (k + 1) * w)
+
+    def gather(name, axis, known, k=None):
+        ref = held["w" + name]
+        spot = tuple(slice(None) if a in known else me[a] for a in axes(name))
+        part = ref.at[spot + (slice(None), chunk(name, k))]
         for at in others(axis):
-            push(name + axis, part, part, at)
-
-    def scatter(name, axis, done):
-        ref = held["g" + name]
-        free = [a for a in AX if a not in done and a != axis]
-        for k, at in enumerate(others(axis)):
-            push("g" + name + axis, ref.at[where_at(at, free)], held["r" + name + axis].at[k], at)
-
-    def add_parts(name, axis, done, finish=None):
-        wait("g" + name + axis)
+            push(("w", name, axis, k), part, part, at)
+
+    def relay(name, axis, nxt, known, k=None):
+        wait(("w", name, axis, k))
+        gather(name, nxt, known + axis, k)
+
+    def arrived(name, k=None):
+        wait(("w", name, "c", k))
+
+    def scatter(name, axis, done, k=None):
         ref, got = held["g" + name], held["r" + name + axis]
-        free = [a for a in AX if a not in done and a != axis]
+        free = [a for a in axes(name) if a not in done and a != axis]
+        cols = (slice(None), chunk(name, k))
+        for n, at in enumerate(others(axis)):
+            spot = tuple(slice(None) if a in free else at[a] for a in axes(name))
+            to = (n,) + (slice(None),) * len(free)
+            push(("g", name, axis, k), ref.at[spot + cols], got.at[to + cols], at)
+
+    def add_parts(name, axis, done, k=None, finish=None):
+        wait(("g", name, axis, k))
+        ref, got = held["g" + name], held["r" + name + axis]
+        free = [a for a in axes(name) if a not in done and a != axis]
+        cols = (slice(None), chunk(name, k))
         total = 1
         for a in free:
             total *= sizes[a]
@@ -454,13 +474,13 @@
             for a in reversed(free):
                 at[a] = rest % sizes[a]
                 rest = rest // sizes[a]
-            spot = tuple(at[a] for a in AX)
+            spot = tuple(at[a] for a in axes(name))
             inner = tuple(at[a] for a in free)
-            acc = ref[spot].astype(F32)
-            for k in range(sizes[axis] - 1):
-                acc = acc + got[(k,) + inner].astype(F32)
+            acc = ref[spot + cols].astype(F32)
+            for n in range(sizes[axis] - 1):
+                acc = acc + got[(n,) + inner + cols].astype(F32)
             if finish is None:
-                ref[spot] = acc.astype(ref.dtype)
+                ref[spot + cols] = acc.astype(ref.dtype)
             else:
                 finish(acc)
             return 0
@@ -470,6 +490,10 @@
         else:
             lax.fori_loop(0, total, one, 0)
 
+    def step(name, axis, nxt, done="", k=None):
+        add_parts(name, axis, done, k)
+        scatter(name, nxt, done + axis, k)
+
     barrier = pltpu.get_barrier_semaphore()
     greet = [at for a in AX for at in others(a)]
     for at in greet:
@@ -481,44 +505,54 @@
     def own(name):
         return held[name].at[me["z"], me["y"], me["c"], x]
 
-    tmp[0 : r.fq.shape[0], :] = r.fq[...].astype(F32)
-    rows = r.fq.shape[0] * 128 // (3 * D)
-    per = 3 * D // 128
-
-    def block64(b, to_high):
+    def block64(b, per, rows, to_high):
         v = tmp[pl.ds(b // 2, rows, stride=per), :]
         return pltpu.roll(v, 64, 1) if (b % 2 == 1) != to_high else v
 
-    for half in range(X):
-        for jj in range(3):
-            for pair in range(HC // 2):
-                h0 = half * HC + 2 * pair
-                low = block64(3 * h0 + jj, False)
-                high = block64(3 * (h0 + 1) + jj, True)
-                at = jj * HW + pair * 128
-                r.sq[half, :, at : at + 128] = jnp.where(lane < 64, low, high).astype(BF16)
-
-    def reshard(src, name, width):
+    def split(src, dst, width, table):
+        n = held[src].shape[0]
+        per = width // 128
+        tmp[0:n, :] = held[src][...].astype(F32)
+        for half in range(X):
+            for m in range(per // X):
+                low, high = table(half, m)
+                low = block64(low, per, n // per, False)
+                high = block64(high, per, n // per, True)
+                dst[half, :, m * 128 : (m + 1) * 128] = jnp.where(lane < 64, low, high).astype(BF16)
+
+    def table_q(half, m):
+        h0 = half * HC + 2 * (m // 3)
+        return 3 * h0 + m % 3, 3 * (h0 + 1) + m % 3
+
+    def table_i(half, m):
+        return 4 * m + half, 4 * m + 2 + half
+
+    def reshard(src, dst, width):
         n = held[src].shape[0]
         k = width // 128
         tmp[0:n, :] = held[src][...].astype(F32)
-        dst = own(name)
         for j in range(k):
             dst[:, j * 128 : (j + 1) * 128] = tmp[pl.ds(j, n // k, stride=k), :].astype(BF16)
 
-    reshard("fd", "wd", D)
-    own("vec")[...] = r.vin[...]
+    split("fq", r.sq, 3 * D, table_q)
+    split("fi", r.si, FF, table_i)
+    reshard("fd", own("wd"), D)
+    own("wv")[...] = r.vin[...]
     own("wq")[...] = r.sq[x]
+    own("wi")[...] = r.si[x]
 
     pl.semaphore_wait(barrier, len(greet))
 
+    rows_mine = pl.ds(pl.multiple_of(x * T, T), T)
+    rows_theirs = pl.ds(pl.multiple_of(xo * T, T), T)
     at_x = others("x")[0]
-    push("wqx", r.sq.at[xo], own("wq"), at_x)
-    gather("vec", "x", "")
-    gather("wd", "x", "")
+    gather("v", "x", "")
+    push("sq", r.sq.at[xo], own("wq"), at_x)
+    push("si", r.si.at[xo], own("wi"), at_x)
+    gather("d", "x", "")
     push("tok", r.tokens, r.tok2, at_x)
-    reshard("fi", "wi", FF)
-    reshard("fo", "wo", D)
+    push("cot", r.cot, r.cots.at[rows_mine, :], at_x)
+    reshard("fo", r.wo.at[me["z"], me["y"], me["c"]], D)
 
     rope = r.rope
     mod = lane % HD
@@ -539,15 +573,16 @@
             + sign * (pltpu.roll(u, 120, 1) * r.sinl[at, :] + pltpu.roll(u, 8, 1) * r.sinh[at, :])
         )
 
-    wait("wqx")
-    gather("wq", "z", "x")
-    gather("wi", "z", "")
-    gather("wo", "z", "")
-    wait("vecx")
-    gather("vec", "y", "x")
-    wait("wdx")
-    gather("wd", "y", "x")
-
+    relay("v", "x", "z", "")
+    wait("sq")
+    gather("q", "z", "x")
+    wait("si")
+    gather("i", "z", "x", 0)
+    gather("i", "z", "x", 1)
+    relay("d", "x", "z", "")
+    gather("o", "z", "", 0)
+    gather("o", "z", "", 1)
+    r.cots[rows_mine, :] = r.cot[...]
     lax.fori_loop(0, S // 32, rope_rows, 0)
 
     RC = 128
@@ -566,37 +601,26 @@
 
     norm_rows(r.tokens, x * T, True)
 
-    wait("wqz")
-    gather("wq", "y", "xz")
-    wait("vecy")
-    gather("vec", "z", "xy")
-    wait("wdy")
-    gather("wd", "z", "xy")
-    wait("wiz")
-    gather("wi", "x", "z")
-    wait("vecz")
-    gather("vec", "c", "xyz")
-    wait("wdz")
-    gather("wd", "c", "xyz")
-    wait("wqy")
-    gather("wq", "c", "xyz")
-    wait("woz")
-    gather("wo", "x", "z")
-    wait("vecc")
+    relay("v", "z", "y", "x")
+    relay("v", "y", "c", "xz")
+    relay("q", "z", "y", "x")
+    arrived("v")
 
     widths = [D // N, D // N, D // N, D // N, 3 * D // N, D // N, FF // N, D // N]
 
     def column(v, n):
         j = iota((1, n), 1)
-        if v != 4:
-            return j
-        hh = (j % HW) // HD
-        return (x * HC + hh) * (3 * HD) + (j // HW) * HD + j % HD
+        if v == 4:
+            head_at = x * HC + 2 * (j // 384) + (j % 128) // HD
+            return head_at * (3 * HD) + ((j % 384) // 128) * HD + j % HD
+        if v == 6:
+            return (j // 64) * 128 + x * 64 + j % 64
+        return j
 
     def lengths(v):
-        return 3 * HW if v == 4 else widths[v] * N
-
-    vec2 = r.vec.reshape(N * 8, 128)
+        return {4: 3 * HW, 6: FH}.get(v, D)
+
+    vec2 = r.wv.reshape(N * 8, 128)
 
     def expand(v):
         n = lengths(v)
@@ -622,48 +646,37 @@
 
         lax.fori_loop(0, T // RC, one, 0)
 
+    def affine_mlp(base):
+        def one(i, _):
+            at = pl.ds(pl.multiple_of(base + i * RC, RC), RC)
+            r.hm[at, :] = (r.n[at, :] * row(2) + row(3)).astype(BF16)
+            return 0
+
+        lax.fori_loop(0, T // RC, one, 0)
+
     affine_attn(x * T)
-
-    def affine_mlp(i, _):
-        at = pl.ds(pl.multiple_of(x * T + i * RC, RC), RC)
-        to = pl.ds(pl.multiple_of(i * RC, RC), RC)
-        r.hm[to, :] = (r.n[at, :] * row(2) + row(3)).astype(BF16)
-        return 0
-
-    lax.fori_loop(0, T // RC, affine_mlp, 0)
-
-    wait("wdc")
-    wd = r.wd.reshape(D, D)
-    for k in range(D // QB):
-        r.do1[:, k * QB : (k + 1) * QB] = mm(
-            r.cot[...], wd[k * QB : (k + 1) * QB, :], NT
-        ).astype(BF16)
-    mine = pl.ds(pl.multiple_of(x * HW, HW), HW)
-    theirs = pl.ds(pl.multiple_of(xo * HW, HW), HW)
-    rows_mine = pl.ds(pl.multiple_of(x * T, T), T)
-    rows_theirs = pl.ds(pl.multiple_of(xo * T, T), T)
-    push("do", r.do1.at[:, theirs], r.do2.at[rows_mine, :], at_x)
-    r.do2[rows_mine, :] = r.do1[:, mine]
-
-    wait("wix")
-    gather("wi", "y", "zx")
-    wait("wox")
-    gather("wo", "y", "zx")
+    affine_mlp(x * T)
+    relay("i", "z", "y", "x", 0)
 
     wait("tok")
     norm_rows(r.tok2, xo * T, False)
     affine_attn(xo * T)
-
-    wait("wqc")
+    affine_mlp(xo * T)
+    relay("i", "z", "y", "x", 1)
+    relay("q", "y", "c", "xz")
+    r.hmt[...] = r.hm[...].T
+    relay("d", "z", "y", "x")
+
+    arrived("q")
     wq = r.wq.reshape(D, 3 * HW)
 
     def qkv_rows(i, _):
         at = pl.ds(pl.multiple_of(i * QB, QB), QB)
         h = r.ha[at, :]
-        for jj, name in enumerate("qkv"):
-            u = mm(h, wq[:, jj * HW : (jj + 1) * HW]) + row(4, HW, jj * HW)
-            for b in range(HW // 128):
-                w = u[:, b * 128 : (b + 1) * 128]
+        u = mm(h, wq[...]) + row(4, 3 * HW)
+        for b in range(HW // 128):
+            for jj, name in enumerate("qkv"):
+                w = u[:, b * 384 + jj * 128 : b * 384 + (jj + 1) * 128]
                 if jj < 2:
                     w = turn(w, at, 1.0)
                 if jj == 0:
@@ -676,9 +689,53 @@
 
     lax.fori_loop(0, S // QB, qkv_rows, 0)
 
-    wait("wiy")
-    gather("wi", "c", "zxy")
-    wait("do")
+    wi = r.wi.reshape(D, FH)
+    wo = r.wo.reshape(FH, D)
+    gi = r.gi.reshape(D, FH)
+    go = r.go.reshape(FH, D)
+    FB = 256
+
+    def ff_cols(b):
+        return pl.ds(pl.multiple_of(b * FB, FB), FB)
+
+    def ff_forward(b, _):
+        cols = ff_cols(b)
+        f = mm(r.hm[...], wi[:, cols]) + r.vrow[6:7, cols]
+        phi = 0.5 + 0.5 * lax.erf(f * (0.5**0.5))
+        r.act[:, cols] = (f * phi).astype(BF16)
+        r.slope[:, cols] = phi + f * (jnp.exp(-0.5 * f * f) * (0.5 / np.pi) ** 0.5)
+        return 0
+
+    relay("i", "y", "c", "xz", 0)
+    relay("o", "z", "y", "", 0)
+    arrived("i", 0)
+    lax.fori_loop(0, FH // FB // 2, ff_forward, 0)
+    relay("i", "y", "c", "xz", 1)
+    relay("o", "z", "y", "", 1)
+    arrived("i", 1)
+    lax.fori_loop(FH // FB // 2, FH // FB, ff_forward, 0)
+    relay("d", "y", "c", "xz")
+    arrived("d")
+
+    wait("cot")
+    wd = r.wd.reshape(D, D)
+    mine = pl.ds(pl.multiple_of(x * HW, HW), HW)
+    r.do2[...] = mm(r.cots[...], wd[mine, :], NT).astype(BF16)
+
+    def out_grad(k):
+        cols = chunk("o", k)
+
+        def one(b, _):
+            at = ff_cols(b)
+            go[at, cols] = mm(r.act[:, at], r.cots[:, cols], TN).astype(BF16)
+            return 0
+
+        lax.fori_loop(0, FH // FB, one, 0)
+        scatter("o", "c", "", k)
+
+    out_grad(0)
+    out_grad(1)
+    relay("o", "y", "c", "z", 0)
 
     r.dk[...] = jnp.zeros_like(r.dk)
     r.dv[...] = jnp.zeros_like(r.dv)
@@ -727,18 +784,18 @@
             r.dv[0:n, lanes] += mm(pb, dom)
         return 0
 
-    lax.fori_loop(0, HC, head, 0)
-
-    push("o", r.ot.at[:, rows_theirs], r.of.at[mine, :], at_x)
-    r.of[mine, :] = r.ot[:, rows_mine]
-    wait("woy")
-    gather("wo", "c", "zxy")
+    def send_o(b):
+        own_rows = slice(b * 128, (b + 1) * 128)
+        to = pl.ds(pl.multiple_of(x * HW + b * 128, 128), 128)
+        push(("o", b), r.ot.at[own_rows, rows_theirs], r.of.at[to, :], at_x)
+        r.of[to, :] = r.ot[own_rows, rows_mine]
 
     r.vg[...] = jnp.zeros_like(r.vg)
-
-    def dqkv_rows(i, _):
-        at = pl.ds(pl.multiple_of(i * QB, QB), QB)
-        for b in range(HW // 128):
+    gq = r.gq.reshape(D, 3 * HW)
+
+    def qkv_back(b):
+        def one(i, _):
+            at = pl.ds(pl.multiple_of(i * QB, QB), QB)
             cols = slice(b * 128, (b + 1) * 128)
             dq = r.dqt[cols, at].T
             out = (
@@ -748,19 +805,72 @@
             )
             for jj in range(3):
                 w = out[jj].astype(BF16)
-                to = slice(jj * HW + b * 128, jj * HW + (b + 1) * 128)
+                to = slice(b * 384 + jj * 128, b * 384 + (jj + 1) * 128)
                 r.dqkv[at, to] = w
                 r.vg[4:5, to] += jnp.sum(w.astype(F32), axis=0, keepdims=True)
+            return 0
+
+        lax.fori_loop(0, S // QB, one, 0)
+        cols = chunk("q", b)
+        for k in range(D // QB):
+            gq[k * QB : (k + 1) * QB, cols] = mm(
+                r.ha[:, k * QB : (k + 1) * QB], r.dqkv[:, cols], TN
+            ).astype(BF16)
+        scatter("q", "c", "", b)
+
+    lax.fori_loop(0, 1, head, 0)
+    relay("o", "y", "c", "z", 1)
+    step("o", "c", "y", "", 0)
+    step("o", "c", "y", "", 1)
+    lax.fori_loop(1, 2, head, 0)
+    send_o(0)
+    qkv_back(0)
+    step("o", "y", "z", "c", 0)
+
+    arrived("o", 0)
+    arrived("o", 1)
+    r.mos[...] = mm(r.act[rows_theirs, :], wo[...]).astype(BF16)
+    push("mo", r.mos, r.mor, at_x)
+    step("o", "y", "z", "c", 1)
+
+    def ff_backward(b, _):
+        cols = ff_cols(b)
+        df = (mm(r.cots[...], wo[cols, :], NT) * r.slope[:, cols]).astype(BF16)
+        r.vg[6:7, cols] = jnp.sum(df.astype(F32), axis=0, keepdims=True)
+        r.df[:, cols] = df
+        gi[:, cols] = mm(r.hmt[...], df).astype(BF16)
         return 0
 
-    lax.fori_loop(0, S // QB, dqkv_rows, 0)
-
-    gq = r.gq.reshape(D, 3 * HW)
-    for k in range(D // QB):
-        gq[k * QB : (k + 1) * QB, :] = mm(
-            r.ha[:, k * QB : (k + 1) * QB], r.dqkv[...], TN
-        ).astype(BF16)
-    scatter("q", "c", "")
+    lax.fori_loop(0, FH // FB // 2, ff_backward, 0)
+    scatter("i", "c", "", 0)
+    step("q", "c", "y", "", 0)
+    lax.fori_loop(FH // FB // 2, FH // FB, ff_backward, 0)
+    scatter("i", "c", "", 1)
+    r.mo[...] = mm(r.act[rows_mine, :], wo[...])
+    step("i", "c", "y", "", 0)
+
+    def dm_rows(i, _):
+        at = pl.ds(pl.multiple_of(i * QB, QB), QB)
+        dm = mm(r.df[at, :], wi[...], NT)
+        r.vg[2:3, 0:D] += jnp.sum(dm * r.n[at, :], axis=0, keepdims=True)
+        r.vg[3:4, 0:D] += jnp.sum(dm, axis=0, keepdims=True)
+        r.um[at, :] = dm * row(2)
+        return 0
+
+    lax.fori_loop(0, S // QB, dm_rows, 0)
+    step("i", "c", "y", "", 1)
+    step("q", "y", "z", "c", 0)
+
+    lax.fori_loop(2, 3, head, 0)
+    step("i", "y", "z", "c", 0)
+    step("i", "y", "z", "c", 1)
+    lax.fori_loop(3, 4, head, 0)
+    send_o(1)
+    half_z = pl.ds(x * (Z // X), Z // X)
+    r.gd.reshape(D, D)[mine, :] = mm(r.ot[...], r.cots[...]).astype(BF16)
+    gd_part = r.gd.at[half_z, :, :, xo]
+    push("gd", gd_part, gd_part, at_x)
+    qkv_back(1)
 
     def dh_rows(base, mine_too):
         def one(i, _):
@@ -769,7 +879,7 @@
             dh = mm(r.dqkv[at, :], wq[...], NT)
             r.vg[0:1, 0:D] += jnp.sum(dh * r.n[at, :], axis=0, keepdims=True)
             r.vg[1:2, 0:D] += jnp.sum(dh, axis=0, keepdims=True)
-            u = dh * row(0)
+            u = dh * row(0) + r.um[at, :]
             if mine_too:
                 r.u[to, :] = u
             else:
@@ -780,51 +890,12 @@
 
     dh_rows(xo * T, False)
     push("u", r.us, r.ur, at_x)
-    add_parts("q", "c", "")
-    scatter("q", "y", "c")
+    step("q", "c", "y", "", 1)
     dh_rows(x * T, True)
 
-    wait("wic")
-    wait("woc")
-    wi = r.wi.reshape(D, FF)
-    wo = r.wo.reshape(FF, D)
-    gi = r.gi.reshape(D, FF)
-    go = r.go.reshape(FF, D)
-    r.hmt[...] = r.hm[...].T
-    r.mo[...] = jnp.zeros_like(r.mo)
-    r.dm[...] = jnp.zeros_like(r.dm)
-    FB = 512
-
-    def ff_block(b, _):
-        cols = pl.ds(pl.multiple_of(b * FB, FB), FB)
-        f = mm(r.hm[...], wi[:, cols]) + r.vrow[6:7, cols]
-        phi = 0.5 + 0.5 * lax.erf(f * (0.5**0.5))
-        a = (f * phi).astype(BF16)
-        slope = phi + f * (jnp.exp(-0.5 * f * f) * (0.5 / np.pi) ** 0.5)
-        df = (mm(r.cot[...], wo[cols, :], NT) * slope).astype(BF16)
-        r.vg[6:7, cols] = jnp.sum(df.astype(F32), axis=0, keepdims=True)
-        r.mo[...] += mm(a, wo[cols, :])
-        r.dm[...] += mm(df, wi[:, cols], NT)
-        go[cols, :] = mm(a, r.cot[...], TN).astype(BF16)
-        gi[:, cols] = mm(r.hmt[...], df).astype(BF16)
-        return 0
-
-    lax.fori_loop(0, FF // FB, ff_block, 0)
-    scatter("i", "c", "")
-    scatter("o", "c", "")
-    add_parts("q", "y", "c")
-    scatter("q", "z", "cy")
-
-    wait("o")
-    r.gd.reshape(D, D)[...] = mm(r.of[...], r.cot[...]).astype(BF16)
-    scatter("d", "c", "")
     g_sum = jnp.sum(r.cot[...].astype(F32), axis=0, keepdims=True)
     r.vg[5:6, 0:D] = g_sum
     r.vg[7:8, 0:D] = g_sum
-    own_n = r.n[rows_mine, :]
-    r.vg[2:3, 0:D] = jnp.sum(r.dm[...] * own_n, axis=0, keepdims=True)
-    r.vg[3:4, 0:D] = jnp.sum(r.dm[...], axis=0, keepdims=True)
-
     gv2 = r.gv.reshape(N * 8, 128)
 
     def collapse(v):
@@ -843,33 +914,53 @@
     for v in range(8):
         collapse(v)
     scatter("v", "c", "")
-
-    add_parts("i", "c", "")
-    scatter("i", "y", "c")
-    add_parts("o", "c", "")
-    scatter("o", "y", "c")
-    add_parts("d", "c", "")
-    scatter("d", "z", "c")
-    add_parts("v", "c", "")
-    scatter("v", "z", "c")
-
+    wait("gd")
+    scatter("d", "c", "x")
+    step("q", "y", "z", "c", 1)
+
+    def flat(out, width, k=None, part=D):
+        per = width // 128
+        n = out.shape[0] // per
+        lo = 0 if k is None else k * (part // 128)
+
+        def put(acc):
+            for j in range(acc.shape[1] // 128):
+                out[pl.ds(lo + j, n, stride=per), :] = acc[:, j * 128 : (j + 1) * 128]
+
+        return put
+
+    add_parts("o", "z", "cy", 0, flat(r.oo, D, 0, CH["o"]))
+    add_parts("o", "z", "cy", 1, flat(r.oo, D, 1, CH["o"]))
+    add_parts("q", "z", "cy", 0)
+    add_parts("i", "z", "cy", 0)
+    add_parts("i", "z", "cy", 1)
+    at_me = (me["z"], me["y"], me["c"])
+    push("si", r.gi.at[at_me + (xo,)], r.xi, at_x)
+    step("v", "c", "y")
+    step("d", "c", "y", "x")
+
+    wait(("o", 0))
+    wait(("o", 1))
+    wait("mo")
     r.out[...] = (
         r.tokens[...].astype(F32)
         + mm(r.of[...], wd[...], TN)
         + row(5)
-        + (r.mo[...] + row(7))
+        + (r.mo[...] + r.mor[...].astype(F32) + row(7))
     ).astype(BF16)
-
-    add_parts("q", "z", "cy")
-    wait_q = r.gq.at[me["z"], me["y"], me["c"], xo]
-    push("gqx", wait_q, r.rqx, at_x)
+    step("v", "y", "z", "c")
+    step("d", "y", "z", "cx")
+    add_parts("q", "z", "cy", 1)
+    push("sq", r.gq.at[at_me + (xo,)], r.xq, at_x)
+    step("v", "z", "x", "cy")
+    add_parts("d", "z", "cyx", None, flat(r.od, D))
 
     wait("u")
 
     def final_rows(i, _):
         at = pl.ds(pl.multiple_of(i * RC, RC), RC)
         far = pl.ds(pl.multiple_of(x * T + i * RC, RC), RC)
-        u = r.u[at, :] + r.ur[at, :].astype(F32) + r.dm[at, :] * row(2)
+        u = r.u[at, :] + r.ur[at, :].astype(F32)
         n = r.n[far, :]
         back = u - jnp.mean(u, axis=-1, keepdims=True) - n * jnp.mean(u * n, axis=-1, keepdims=True)
         r.gtok[at, :] = (r.cot[at, :].astype(F32) + back * r.scale[at, 0:1]).astype(BF16)
@@ -877,59 +968,38 @@
 
     lax.fori_loop(0, T // RC, final_rows, 0)
 
-    add_parts("i", "y", "c")
-    scatter("i", "x", "cy")
-    add_parts("o", "y", "c")
-    scatter("o", "x", "cy")
-    add_parts("d", "z", "c")
-    scatter("d", "y", "cz")
-    add_parts("v", "z", "c")
-    scatter("v", "y", "cz")
-    add_parts("d", "y", "cz")
-    scatter("d", "x", "czy")
-    add_parts("v", "y", "cz")
-    scatter("v", "x", "czy")
-    add_parts("i", "x", "cy")
-    scatter("i", "z", "cyx")
-    add_parts("o", "x", "cy")
-    scatter("o", "z", "cyx")
-
-    def flat(name, width):
-        out = held[name]
-        k = width // 128
-        n = out.shape[0] // k
-
-        def put(acc):
-            for j in range(k):
-                out[pl.ds(j, n, stride=k), :] = acc[:, j * 128 : (j + 1) * 128]
-
-        return put
-
-    wait("gqx")
-    half_own = r.gq[me["z"], me["y"], me["c"], x].astype(F32)
-    half_got = r.rqx[...].astype(F32)
-    lo_half = jnp.where(x == 0, half_own, half_got)
-    hi_half = jnp.where(x == 0, half_got, half_own)
-    halves = (lo_half, hi_half)
-
-    def piece(b, to_high):
+    def join(mine_ref, got, out, width, place):
+        per = width // 128
+        n = out.shape[0] // per
+        here = mine_ref[at_me + (x,)].astype(F32)
+        there = got[...].astype(F32)
+        halves = (jnp.where(x == 0, here, there), jnp.where(x == 0, there, here))
+
+        def piece(b, to_high):
+            half, m, odd = place(b)
+            v = halves[half][:, m * 128 : (m + 1) * 128]
+            return pltpu.roll(v, 64, 1) if odd != to_high else v
+
+        for j in range(per):
+            both = jnp.where(lane < 64, piece(2 * j, False), piece(2 * j + 1, True))
+            out[pl.ds(j, n, stride=per), :] = both
+
+    def place_q(b):
         h, jj = b // 3, b % 3
-        half, hh = h // HC, h % HC
-        at = jj * HW + (hh // 2) * 128
-        v = halves[half][:, at : at + 128]
-        return pltpu.roll(v, 64, 1) if (hh % 2 == 1) != to_high else v
-
-    for j in range(per):
-        both = jnp.where(lane < 64, piece(2 * j, False), piece(2 * j + 1, True))
-        r.oq[pl.ds(j, rows, stride=per), :] = both
+        return h // HC, (h % HC) // 2 * 3 + jj, h % 2 == 1
+
+    def place_i(b):
+        return b % 2, b // 4, (b // 2) % 2 == 1
+
+    wait("si")
+    join(r.gi, r.xi, r.oi, FF, place_i)
+    wait("sq")
+    join(r.gq, r.xq, r.oq, 3 * D, place_q)
 
     def put_vec(acc):
         r.ov[...] = acc
 
-    add_parts("d", "x", "czy", flat("od", D))
-    add_parts("v", "x", "czy", put_vec)
-    add_parts("i", "z", "cyx", flat("oi", FF))
-    add_parts("o", "z", "cyx", flat("oo", D))
+    add_parts("v", "x", "cyz", None, put_vec)
 
 
 def rope_table(length):
@@ -953,39 +1023,44 @@
     flats = [w.reshape(-1, 128) for w in weights]
     full = dict(z=Z, y=Y, c=C, x=X)
 
-    def parts(axis, done, slab, dtype, last=False):
-        free = [full[a] for a in AX if a not in done and a != axis]
+    FH = FF // X
+
+    def parts(name, axis, done, slab, dtype):
+        free = [full[a] for a in AX if a not in done and a != axis and (a != "x" or name != "o")]
         return pltpu.VMEM((full[axis] - 1, *free, *slab), dtype)
 
     slabs = {
         "q": (D // N, 3 * HW),
         "d": (D // N, D),
-        "i": (D // N, FF),
+        "i": (D // N, FH),
         "o": (FF // N, D),
         "v": (8, 128),
     }
-    orders = {"q": "cyz", "d": "czyx", "i": "cyxz", "o": "cyxz", "v": "czyx"}
+    orders = {"q": "cyz", "d": "cyz", "i": "cyz", "o": "cyz", "v": "cyzx"}
     keep = types.SimpleNamespace()
     scratch = vars(keep)
     for k, slab in slabs.items():
         kind = F32 if k == "v" else BF16
-        scratch["vec" if k == "v" else "w" + k] = pltpu.VMEM((Z, Y, C, X, *slab), kind)
-        scratch["g" + k] = pltpu.VMEM((Z, Y, C, X, *slab), kind)
+        devs = (Z, Y, C) if k == "o" else (Z, Y, C, X)
+        scratch["w" + k] = pltpu.VMEM((*devs, *slab), kind)
+        scratch["g" + k] = pltpu.VMEM((*devs, *slab), kind)
         for n, axis in enumerate(orders[k]):
-            scratch["r" + k + axis] = parts(axis, orders[k][:n], slab, kind)
-    keep.rqx = pltpu.VMEM(slabs["q"], BF16)
+            done = orders[k][:n] + ("x" if k == "d" else "")
+            scratch["r" + k + axis] = parts(k, axis, done, slab, kind)
+    keep.xq = pltpu.VMEM(slabs["q"], BF16)
+    keep.xi = pltpu.VMEM(slabs["i"], BF16)
     keep.sq = pltpu.VMEM((X, *slabs["q"]), BF16)
+    keep.si = pltpu.VMEM((X, *slabs["i"]), BF16)
     keep.tmp = pltpu.VMEM((max(f.shape[0] for f in flats), 128), F32)
     keep.cos = keep.sinl = keep.sinh = pltpu.VMEM((S, 128), F32)
     keep.tok2 = pltpu.VMEM((T, D), BF16)
+    keep.cots = pltpu.VMEM((S, D), BF16)
     keep.n = pltpu.VMEM((S, D), F32)
     keep.scale = pltpu.VMEM((T, 128), F32)
-    keep.vrow = pltpu.VMEM((8, FF), F32)
-    keep.vg = pltpu.VMEM((8, FF), F32)
-    keep.ha = pltpu.VMEM((S, D), BF16)
-    keep.hm = pltpu.VMEM((T, D), BF16)
-    keep.hmt = pltpu.VMEM((D, T), BF16)
-    keep.do1 = pltpu.VMEM((T, D), BF16)
+    keep.vrow = pltpu.VMEM((8, FH), F32)
+    keep.vg = pltpu.VMEM((8, FH), F32)
+    keep.ha = keep.hm = pltpu.VMEM((S, D), BF16)
+    keep.hmt = pltpu.VMEM((D, S), BF16)
     keep.q = keep.k = keep.v = keep.do2 = pltpu.VMEM((S, HW), BF16)
     keep.kt = keep.vt = keep.ot = pltpu.VMEM((HW, S), BF16)
     keep.dqt = pltpu.VMEM((HW, S), F32)
@@ -997,12 +1072,12 @@
     keep.ds = pltpu.VMEM((S, QB), BF16)
     keep.dqkv = pltpu.VMEM((S, 3 * HW), BF16)
     keep.of = pltpu.VMEM((D, T), BF16)
-    keep.u = pltpu.VMEM((T, D), F32)
-    keep.us = pltpu.VMEM((T, D), BF16)
-    keep.ur = pltpu.VMEM((T, D), BF16)
-    keep.mo = pltpu.VMEM((T, D), F32)
-    keep.dm = pltpu.VMEM((T, D), F32)
-    copies = 4 * (2 * (Z - 1) + 2 * 3) + 2 * (Z + 2) + 16
+    keep.act = keep.df = pltpu.VMEM((S, FH), BF16)
+    keep.slope = pltpu.VMEM((S, FH), F32)
+    keep.um = pltpu.VMEM((S, D), F32)
+    keep.u = keep.mo = pltpu.VMEM((T, D), F32)
+    keep.us = keep.ur = keep.mos = keep.mor = pltpu.VMEM((T, D), BF16)
+    copies = 128
     keep.send = pltpu.SemaphoreType.DMA((copies,))
     keep.recv = pltpu.SemaphoreType.DMA((copies,))
     ins = "tokens cot fq fd".split() + "fi fo vin rope".split()
@@ -1055,7 +1130,7 @@
 
 def solution(mesh):
     n_seq, n_ctx = mesh.shape["seq"], mesh.shape["ctx"]
-    if n_ctx != 2 or n_seq % 4 or (D // (n_seq * n_ctx)) % 16:
+    if n_ctx != 2 or n_seq % 8 or (D // (n_seq * n_ctx)) % 16:
         return general(mesh)
     sizes = {"z": n_seq // 4, "y": 2, "c": 2, "x": n_ctx}
     flat = P(("seq", "ctx"))

time: 132 us -> 103 us (0.78)
  Pallas kernels: 120 us -> 90.8 us
    pallas_call x1, Pallas kernels: 120 us -> 90.8 us  [layer(): pl.pallas_call(functools.partial(fused, sizes, names), out_shape=list(out...]
where the time goes in v2:
time: 103 us
  Pallas kernels  90.8 us (88%)
  local copies, waits for them, and re-layouts  10.8 us (10%)
    pallas_call x1, Pallas kernels, layer(): pl.pallas_call(functools.partial(fused, sizes, names), out_shape=list(out...  90.8 us
    unnamed x34, local copies, waits for them, and re-layouts  9.2 us

profile of v2, /device:TPU:0, one launch (start us, length us, event | category | flops | bytes accessed | tf_op | source)
XLA Modules:
  0.0 103.0 jit_solution(1701941422380529656)
XLA Ops:
  0.6 0.0 copy-start.6
  0.7 0.0 copy-start.7
  0.7 0.6 copy-done.6
  1.3 0.0 copy-done.7
  1.3 0.0 copy-start.8
  1.3 0.0 copy-start.9
  1.3 0.6 copy-done.8
  2.0 0.0 copy-done.9
  2.0 0.0 copy-start.10
  2.0 0.0 copy-start.11
  2.0 0.6 copy-done.10
  2.7 0.0 copy-done.11
  2.7 0.0 copy-start.12
  2.7 0.0 copy-start.13
  2.7 0.6 copy-done.12
  3.3 0.0 copy-done.13
  3.4 0.6 stack.46.refs_6_
  4.0 90.8 %layer.1 = (bf16[512,512]{1,0:T(8,128)(2,1)}, bf16[512,512]{1,0:T(8,128)(2,1)}, f32[192,128]{1,0:T(8,128)}, f32[64,128]{1,0:T(8,128)}, f32[256,128]{1,0:T(8,128)}, /*index=5*/f32[256,128]{1,0:T(8,128)}, f32[8,128]{1,0:T(8,128)}) custom-call(bf16[512,512]{1,0:T(8,128)(2,1)} %bitcast.44, bf16[512,512]{1,0:T(8,128)(2,1)} %bitcast.45, ...), custom_call_target="tpu_custom_call" | custom-call | tf_op jit(solution)/shard_map/layer/pallas_call | solution.py:1095
  94.8 0.0 copy-start.5
  94.8 0.7 copy-done.5
  95.5 0.5 slice_bitcast_fusion.3
  96.0 0.5 slice_bitcast_fusion.1
  96.5 0.5 slice_bitcast_fusion
  97.1 0.0 copy-start
  97.1 1.9 %copy.35 = bf16[1,512,512]{2,1,0:T(8,128)(2,1)} copy(bf16[1,512,512]{2,1,0:T(8,128)(2,1)} %bitcast.47) | data formatting | bytes 1048576
  99.0 0.0 copy-done
  99.0 0.0 copy-start.3
  99.0 0.8 copy.36
  99.8 0.2 copy-done.3
  100.0 0.0 copy-start.4
  100.0 0.0 copy-start.2
  100.0 0.6 copy.37
  100.6 0.1 copy-done.4
  100.7 0.6 copy.38
  101.3 0.0 copy-done.2
  101.3 0.0 copy-start.1
  101.3 0.7 copy.39
  102.0 0.3 copy-done.1
  102.3 0.7 copy.40
  (5 shorter events, 0.1 us)
Async XLA Ops:
  0.6 0.7 copy-start.6
  0.7 0.7 copy-start.7
  1.3 0.7 copy-start.8
  1.3 0.7 copy-start.9
  2.0 0.7 copy-start.10
  2.0 0.7 copy-start.11
  2.7 0.7 copy-start.12
  2.7 0.7 copy-start.13
  94.8 0.7 copy-start.5
  97.1 1.9 %copy-start = (bf16[512,512]{1,0:T(8,128)(2,1)S(1)}, bf16[512,512]{1,0:T(8,128)(2,1)}, u32[]{:S(2)}) copy-start(bf16[512,512]{1,0:T(8,128)(2,1)} %get-tuple-element.22) | copy-start | bytes 1572868
  99.0 1.0 copy-start.3
  100.0 0.8 copy-start.4
  100.0 1.4 %copy-start.2 = (f32[256,128]{1,0:T(8,128)S(1)}, f32[256,128]{1,0:T(8,128)}, u32[]{:S(2)}) copy-start(f32[256,128]{1,0:T(8,128)} %get-tuple-element.26) | copy-start | bytes 393220
  101.3 1.0 copy-start.1

commit v3 on v2

--- a/solution.py
+++ b/solution.py
@@ -537,7 +537,11 @@
     split("fq", r.sq, 3 * D, table_q)
     split("fi", r.si, FF, table_i)
     reshard("fd", own("wd"), D)
-    own("wv")[...] = r.vin[...]
+    vecs = own("wv")
+    vecs[...] = jnp.zeros_like(vecs)
+    for v in range(8):
+        vin = held["v%d" % v]
+        vecs[v : v + 1, 0 : vin.shape[1]] = vin[...].astype(F32)
     own("wq")[...] = r.sq[x]
     own("wi")[...] = r.si[x]
 
@@ -575,14 +579,14 @@
 
     relay("v", "x", "z", "")
     wait("sq")
-    gather("q", "z", "x")
+    gather("q", "z", "x", 0)
+    gather("q", "z", "x", 1)
+    relay("d", "x", "z", "")
     wait("si")
     gather("i", "z", "x", 0)
     gather("i", "z", "x", 1)
-    relay("d", "x", "z", "")
     gather("o", "z", "", 0)
     gather("o", "z", "", 1)
-    r.cots[rows_mine, :] = r.cot[...]
     lax.fori_loop(0, S // 32, rope_rows, 0)
 
     RC = 128
@@ -602,8 +606,9 @@
     norm_rows(r.tokens, x * T, True)
 
     relay("v", "z", "y", "x")
+    relay("q", "z", "y", "x", 0)
     relay("v", "y", "c", "xz")
-    relay("q", "z", "y", "x")
+    relay("q", "z", "y", "x", 1)
     arrived("v")
 
     widths = [D // N, D // N, D // N, D // N, 3 * D // N, D // N, FF // N, D // N]
@@ -655,7 +660,10 @@
         lax.fori_loop(0, T // RC, one, 0)
 
     affine_attn(x * T)
+    relay("d", "z", "y", "x")
+    relay("q", "y", "c", "xz", 0)
     affine_mlp(x * T)
+    relay("q", "y", "c", "xz", 1)
     relay("i", "z", "y", "x", 0)
 
     wait("tok")
@@ -663,20 +671,16 @@
     affine_attn(xo * T)
     affine_mlp(xo * T)
     relay("i", "z", "y", "x", 1)
-    relay("q", "y", "c", "xz")
-    r.hmt[...] = r.hm[...].T
-    relay("d", "z", "y", "x")
-
-    arrived("q")
+    relay("d", "y", "c", "xz")
+
     wq = r.wq.reshape(D, 3 * HW)
 
-    def qkv_rows(i, _):
-        at = pl.ds(pl.multiple_of(i * QB, QB), QB)
-        h = r.ha[at, :]
-        u = mm(h, wq[...]) + row(4, 3 * HW)
-        for b in range(HW // 128):
+    def qkv(b):
+        def one(i, _):
+            at = pl.ds(pl.multiple_of(i * QB, QB), QB)
+            u = mm(r.ha[at, :], wq[:, chunk("q", b)]) + row(4, 384, b * 384)
             for jj, name in enumerate("qkv"):
-                w = u[:, b * 384 + jj * 128 : b * 384 + (jj + 1) * 128]
+                w = u[:, jj * 128 : (jj + 1) * 128]
                 if jj < 2:
                     w = turn(w, at, 1.0)
                 if jj == 0:
@@ -685,67 +689,27 @@
                 held[name][at, b * 128 : (b + 1) * 128] = w
                 if jj >= 1:
                     held[name + "t"][b * 128 : (b + 1) * 128, at] = w.T
-        return 0
-
-    lax.fori_loop(0, S // QB, qkv_rows, 0)
-
-    wi = r.wi.reshape(D, FH)
-    wo = r.wo.reshape(FH, D)
-    gi = r.gi.reshape(D, FH)
-    go = r.go.reshape(FH, D)
-    FB = 256
-
-    def ff_cols(b):
-        return pl.ds(pl.multiple_of(b * FB, FB), FB)
-
-    def ff_forward(b, _):
-        cols = ff_cols(b)
-        f = mm(r.hm[...], wi[:, cols]) + r.vrow[6:7, cols]
-        phi = 0.5 + 0.5 * lax.erf(f * (0.5**0.5))
-        r.act[:, cols] = (f * phi).astype(BF16)
-        r.slope[:, cols] = phi + f * (jnp.exp(-0.5 * f * f) * (0.5 / np.pi) ** 0.5)
-        return 0
-
-    relay("i", "y", "c", "xz", 0)
-    relay("o", "z", "y", "", 0)
-    arrived("i", 0)
-    lax.fori_loop(0, FH // FB // 2, ff_forward, 0)
-    relay("i", "y", "c", "xz", 1)
-    relay("o", "z", "y", "", 1)
-    arrived("i", 1)
-    lax.fori_loop(FH // FB // 2, FH // FB, ff_forward, 0)
-    relay("d", "y", "c", "xz")
+            return 0
+
+        arrived("q", b)
+        lax.fori_loop(0, S // QB, one, 0)
+
+    qkv(0)
+    qkv(1)
     arrived("d")
-
-    wait("cot")
     wd = r.wd.reshape(D, D)
     mine = pl.ds(pl.multiple_of(x * HW, HW), HW)
-    r.do2[...] = mm(r.cots[...], wd[mine, :], NT).astype(BF16)
-
-    def out_grad(k):
-        cols = chunk("o", k)
-
-        def one(b, _):
-            at = ff_cols(b)
-            go[at, cols] = mm(r.act[:, at], r.cots[:, cols], TN).astype(BF16)
-            return 0
-
-        lax.fori_loop(0, FH // FB, one, 0)
-        scatter("o", "c", "", k)
-
-    out_grad(0)
-    out_grad(1)
-    relay("o", "y", "c", "z", 0)
+    r.do2[rows_mine, :] = mm(r.cot[...], wd[mine, :], NT).astype(BF16)
 
     r.dk[...] = jnp.zeros_like(r.dk)
     r.dv[...] = jnp.zeros_like(r.dv)
     causal = iota((QB, QB), 0) <= iota((QB, QB), 1)
 
-    def head(h, _):
+    def head(blocks, h, _):
         lanes = pl.ds(pl.multiple_of((h // 2) * 128, 128), 128)
         ours = (lane // HD) == h % 2
         head_rows = pl.ds(pl.multiple_of(h * HD, HD), HD)
-        for i in range(S // QB):
+        for i in blocks:
             here = slice(i * QB, (i + 1) * QB)
             qm = jnp.where(ours, r.q[here, lanes], jnp.zeros((), BF16))
             dom = jnp.where(ours, r.do2[here, lanes], jnp.zeros((), BF16))
@@ -784,6 +748,62 @@
             r.dv[0:n, lanes] += mm(pb, dom)
         return 0
 
+    per_x = T // QB
+
+    def attend(theirs, first, last):
+        for k in range(X):
+            at = (1 - k if theirs else k) * per_x
+            run = functools.partial(head, range(at, at + per_x))
+
+            @pl.when(x == k)
+            def _():
+                lax.fori_loop(first, last, run, 0)
+
+    attend(False, 0, 2)
+    relay("i", "y", "c", "xz", 0)
+    relay("o", "z", "y", "", 0)
+    attend(False, 2, 4)
+    relay("i", "y", "c", "xz", 1)
+    r.hmt[...] = r.hm[...].T
+
+    wi = r.wi.reshape(D, FH)
+    wo = r.wo.reshape(FH, D)
+    gi = r.gi.reshape(D, FH)
+    go = r.go.reshape(FH, D)
+    FB = 256
+
+    def ff_cols(b):
+        return pl.ds(pl.multiple_of(b * FB, FB), FB)
+
+    def ff_forward(b, _):
+        cols = ff_cols(b)
+        f = mm(r.hm[...], wi[:, cols]) + r.vrow[6:7, cols]
+        phi = 0.5 + 0.5 * lax.erf(f * (0.5**0.5))
+        r.act[:, cols] = (f * phi).astype(BF16)
+        r.slope[:, cols] = phi + f * (jnp.exp(-0.5 * f * f) * (0.5 / np.pi) ** 0.5)
+        return 0
+
+    arrived("i", 0)
+    lax.fori_loop(0, FH // FB // 2, ff_forward, 0)
+    relay("o", "z", "y", "", 1)
+    arrived("i", 1)
+    lax.fori_loop(FH // FB // 2, FH // FB, ff_forward, 0)
+    relay("o", "y", "c", "z", 0)
+
+    wait("cot")
+    r.cots[rows_mine, :] = r.cot[...]
+    r.do2[rows_theirs, :] = mm(r.cots[rows_theirs, :], wd[mine, :], NT).astype(BF16)
+
+    def out_grad(b, _):
+        at = ff_cols(b)
+        go[at, :] = mm(r.act[:, at], r.cots[...], TN).astype(BF16)
+        return 0
+
+    lax.fori_loop(0, FH // FB, out_grad, 0)
+    scatter("o", "c", "", 0)
+    scatter("o", "c", "", 1)
+    relay("o", "y", "c", "z", 1)
+
     def send_o(b):
         own_rows = slice(b * 128, (b + 1) * 128)
         to = pl.ds(pl.multiple_of(x * HW + b * 128, 128), 128)
@@ -818,20 +838,12 @@
             ).astype(BF16)
         scatter("q", "c", "", b)
 
-    lax.fori_loop(0, 1, head, 0)
-    relay("o", "y", "c", "z", 1)
-    step("o", "c", "y", "", 0)
-    step("o", "c", "y", "", 1)
-    lax.fori_loop(1, 2, head, 0)
-    send_o(0)
-    qkv_back(0)
-    step("o", "y", "z", "c", 0)
-
     arrived("o", 0)
     arrived("o", 1)
     r.mos[...] = mm(r.act[rows_theirs, :], wo[...]).astype(BF16)
     push("mo", r.mos, r.mor, at_x)
-    step("o", "y", "z", "c", 1)
+    step("o", "c", "y", "", 0)
+    step("o", "c", "y", "", 1)
 
     def ff_backward(b, _):
         cols = ff_cols(b)
@@ -843,11 +855,9 @@
 
     lax.fori_loop(0, FH // FB // 2, ff_backward, 0)
     scatter("i", "c", "", 0)
-    step("q", "c", "y", "", 0)
     lax.fori_loop(FH // FB // 2, FH // FB, ff_backward, 0)
     scatter("i", "c", "", 1)
     r.mo[...] = mm(r.act[rows_mine, :], wo[...])
-    step("i", "c", "y", "", 0)
 
     def dm_rows(i, _):
         at = pl.ds(pl.multiple_of(i * QB, QB), QB)
@@ -858,13 +868,17 @@
         return 0
 
     lax.fori_loop(0, S // QB, dm_rows, 0)
+    step("i", "c", "y", "", 0)
     step("i", "c", "y", "", 1)
-    step("q", "y", "z", "c", 0)
-
-    lax.fori_loop(2, 3, head, 0)
+    step("o", "y", "z", "c", 0)
+    step("o", "y", "z", "c", 1)
+
+    attend(True, 0, 2)
+    send_o(0)
+    qkv_back(0)
     step("i", "y", "z", "c", 0)
     step("i", "y", "z", "c", 1)
-    lax.fori_loop(3, 4, head, 0)
+    attend(True, 2, 4)
     send_o(1)
     half_z = pl.ds(x * (Z // X), Z // X)
     r.gd.reshape(D, D)[mine, :] = mm(r.ot[...], r.cots[...]).astype(BF16)
@@ -890,6 +904,7 @@
 
     dh_rows(xo * T, False)
     push("u", r.us, r.ur, at_x)
+    step("q", "c", "y", "", 0)
     step("q", "c", "y", "", 1)
     dh_rows(x * T, True)
 
@@ -916,6 +931,7 @@
     scatter("v", "c", "")
     wait("gd")
     scatter("d", "c", "x")
+    step("q", "y", "z", "c", 0)
     step("q", "y", "z", "c", 1)
 
     def flat(out, width, k=None, part=D):
@@ -1011,6 +1027,13 @@
     return np.stack([np.cos(high), np.sin(high), np.cos(low), np.sin(low)]).astype(np.float32)
 
 
+def hand_over(*refs):
+    for src, dst in zip(refs[:6], refs[7:13]):
+        dst[...] = src[...]
+    for v, dst in enumerate(refs[13:]):
+        dst[...] = refs[6][v : v + 1, 0 : dst.shape[1]]
+
+
 def layer(sizes, tokens, cotangent, *params):
     Z, Y, C, X = (sizes[a] for a in AX)
     N = Z * Y * C * X
@@ -1019,7 +1042,6 @@
     HW = HEADS // X * HD
     vectors = [params[i] for i in (0, 1, 2, 3, 5, 7, 9, 11)]
     weights = [params[i] for i in (4, 6, 8, 10)]
-    vin = jnp.stack([jnp.pad(v.astype(F32), (0, 128 - v.shape[0])) for v in vectors])
     flats = [w.reshape(-1, 128) for w in weights]
     full = dict(z=Z, y=Y, c=C, x=X)
 
@@ -1080,7 +1102,7 @@
     copies = 128
     keep.send = pltpu.SemaphoreType.DMA((copies,))
     keep.recv = pltpu.SemaphoreType.DMA((copies,))
-    ins = "tokens cot fq fd".split() + "fi fo vin rope".split()
+    ins = "tokens cot fq fd".split() + "fi fo rope".split() + ["v%d" % v for v in range(8)]
     outs = dict(
         out=jax.ShapeDtypeStruct((T, D), BF16),
         gtok=jax.ShapeDtypeStruct((T, D), BF16),
@@ -1106,10 +1128,19 @@
         tokens.reshape(T, D),
         cotangent.reshape(T, D),
         *flats,
-        vin,
         jnp.asarray(rope_table(S)),
-    )
-    v = [gv[i, : p.shape[0]] for i, p in enumerate(vectors)]
+        *[v.reshape(1, -1) for v in vectors],
+    )
+    shapes = [jax.ShapeDtypeStruct(a.shape, a.dtype) for a in (out, gtok, gq, gd, gi, go)]
+    shapes += [jax.ShapeDtypeStruct((1, p.shape[0]), F32) for p in vectors]
+    out, gtok, gq, gd, gi, go, *v = pl.pallas_call(
+        hand_over,
+        out_shape=shapes,
+        in_specs=[vmem] * 7,
+        out_specs=[vmem] * len(shapes),
+        name="results",
+    )(out, gtok, gq, gd, gi, go, gv)
+    v = [a.reshape(-1) for a in v]
     return (
         out.reshape(tokens.shape),
         gtok.reshape(tokens.shape),

time: 103 us -> 98.1 us (0.952)
  local copies, waits for them, and re-layouts: 10.8 us -> 0 us
  Pallas kernels: 90.8 us -> 97.1 us
    unnamed x34 -> x0, local copies, waits for them, and re-layouts: 9.2 us -> none
    pallas_call x1, Pallas kernels: 90.8 us -> 94.6 us  [layer(): pl.pallas_call(functools.partial(fused, sizes, names), out_shape=list(out...]
    pallas_call x0 -> x1, Pallas kernels: none -> 2.5 us  [layer(): pl.pallas_call(hand_over, out_shape=shapes, in_specs=[vmem] * 7, out_spec...]
    squeeze x3 -> x0, local copies, waits for them, and re-layouts: 1.56 us -> none  [layer(): v = [gv[i, :p.shape[0]] for i, p in enumerate(vectors)]]
where the time goes in v3:
time: 98.1 us; the launch traced here: 98 us
  Pallas kernels  97.1 us (99%)
    pallas_call x1, Pallas kernels, layer(): pl.pallas_call(functools.partial(fused, sizes, names), out_shape=list(out...  94.6 us
    pallas_call x1, Pallas kernels, layer(): pl.pallas_call(hand_over, out_shape=shapes, in_specs=[vmem] * 7, out_spec...  2.5 us

profile of v3, /device:TPU:0, one launch (start us, length us, event | category | flops | bytes accessed | tf_op | source)
XLA Modules:
  0.0 98.0 jit_solution(4681117928854177487)
XLA Ops:
  0.7 94.6 %layer.1 = (bf16[512,512]{1,0:T(8,128)(2,1)}, bf16[512,512]{1,0:T(8,128)(2,1)}, f32[192,128]{1,0:T(8,128)}, f32[64,128]{1,0:T(8,128)}, f32[256,128]{1,0:T(8,128)}, /*index=5*/f32[256,128]{1,0:T(8,128)}, f32[8,128]{1,0:T(8,128)}) custom-call(bf16[512,512]{1,0:T(8,128)(2,1)} %bitcast.28, bf16[512,512]{1,0:T(8,128)(2,1)} %bitcast.29, ...), custom_call_target="tpu_custom_call" | custom-call | tf_op jit(solution)/shard_map/layer/pallas_call | solution.py:1117
  95.3 2.5 %results.1 = (bf16[512,512]{1,0:T(8,128)(2,1)}, bf16[512,512]{1,0:T(8,128)(2,1)}, f32[192,128]{1,0:T(8,128)}, f32[64,128]{1,0:T(8,128)}, f32[256,128]{1,0:T(8,12...) custom-call(bf16[512,512]{1,0:T(8,128)(2,1)} %get-tuple-element.35.r, ...), custom_call_target="tpu_custom_call" | custom-call | tf_op jit(solution)/shard_map/results/pallas_call | solution.py:1136

commit v4 on v3

--- a/solution.py
+++ b/solution.py
@@ -664,13 +664,12 @@
     relay("q", "y", "c", "xz", 0)
     affine_mlp(x * T)
     relay("q", "y", "c", "xz", 1)
-    relay("i", "z", "y", "x", 0)
 
     wait("tok")
     norm_rows(r.tok2, xo * T, False)
     affine_attn(xo * T)
     affine_mlp(xo * T)
-    relay("i", "z", "y", "x", 1)
+    relay("i", "z", "y", "x", 0)
     relay("d", "y", "c", "xz")
 
     wq = r.wq.reshape(D, 3 * HW)
@@ -695,6 +694,7 @@
         lax.fori_loop(0, S // QB, one, 0)
 
     qkv(0)
+    relay("i", "z", "y", "x", 1)
     qkv(1)
     arrived("d")
     wd = r.wd.reshape(D, D)
@@ -721,24 +721,21 @@
                 r.st[j] = st
                 part = jnp.max(st, axis=0, keepdims=True)
                 top = part if top is None else jnp.maximum(top, part)
-            total = None
+            total = du = None
             for j in range(i + 1):
                 e = jnp.exp(r.st[j] - top)
                 r.st[j] = e
-                part = jnp.sum(e, axis=0, keepdims=True)
+                dp = mm(r.v[j * QB : (j + 1) * QB, lanes], dom, NT)
+                r.dp[j] = dp
+                part, both = (jnp.sum(w, axis=0, keepdims=True) for w in (e, e * dp))
                 total = part if total is None else total + part
+                du = both if du is None else du + both
             scale = 1.0 / total
-            delta = None
+            delta = du * scale
             for j in range(i + 1):
                 p = r.st[j] * scale
-                r.st[j] = p
                 r.pb[j * QB : (j + 1) * QB, :] = p.astype(BF16)
-                dp = mm(r.v[j * QB : (j + 1) * QB, lanes], dom, NT)
-                r.dp[j] = dp
-                part = jnp.sum(p * dp, axis=0, keepdims=True)
-                delta = part if delta is None else delta + part
-            for j in range(i + 1):
-                ds = r.st[j] * (r.dp[j] - delta)
+                ds = p * (r.dp[j] - delta)
                 r.ds[j * QB : (j + 1) * QB, :] = ds.astype(BF16)
             n = (i + 1) * QB
             pb, ds = r.pb[0:n, :], r.ds[0:n, :]
@@ -788,7 +785,6 @@
     relay("o", "z", "y", "", 1)
     arrived("i", 1)
     lax.fori_loop(FH // FB // 2, FH // FB, ff_forward, 0)
-    relay("o", "y", "c", "z", 0)
 
     wait("cot")
     r.cots[rows_mine, :] = r.cot[...]
@@ -802,7 +798,7 @@
     lax.fori_loop(0, FH // FB, out_grad, 0)
     scatter("o", "c", "", 0)
     scatter("o", "c", "", 1)
-    relay("o", "y", "c", "z", 1)
+    relay("o", "y", "c", "z", 0)
 
     def send_o(b):
         own_rows = slice(b * 128, (b + 1) * 128)
@@ -838,12 +834,27 @@
             ).astype(BF16)
         scatter("q", "c", "", b)
 
+    attend(True, 0, 2)
+    relay("o", "y", "c", "z", 1)
+    step("o", "c", "y", "", 0)
+    step("o", "c", "y", "", 1)
+    send_o(0)
+    qkv_back(0)
+
     arrived("o", 0)
     arrived("o", 1)
     r.mos[...] = mm(r.act[rows_theirs, :], wo[...]).astype(BF16)
     push("mo", r.mos, r.mor, at_x)
-    step("o", "c", "y", "", 0)
-    step("o", "c", "y", "", 1)
+    attend(True, 2, 4)
+    send_o(1)
+    half_z = pl.ds(x * (Z // X), Z // X)
+    r.gd.reshape(D, D)[mine, :] = mm(r.ot[...], r.cots[...]).astype(BF16)
+    gd_part = r.gd.at[half_z, :, :, xo]
+    push("gd", gd_part, gd_part, at_x)
+    step("q", "c", "y", "", 0)
+    step("o", "y", "z", "c", 0)
+    step("o", "y", "z", "c", 1)
+    qkv_back(1)
 
     def ff_backward(b, _):
         cols = ff_cols(b)
@@ -855,45 +866,23 @@
 
     lax.fori_loop(0, FH // FB // 2, ff_backward, 0)
     scatter("i", "c", "", 0)
+    step("q", "c", "y", "", 1)
     lax.fori_loop(FH // FB // 2, FH // FB, ff_backward, 0)
     scatter("i", "c", "", 1)
-    r.mo[...] = mm(r.act[rows_mine, :], wo[...])
-
-    def dm_rows(i, _):
-        at = pl.ds(pl.multiple_of(i * QB, QB), QB)
-        dm = mm(r.df[at, :], wi[...], NT)
-        r.vg[2:3, 0:D] += jnp.sum(dm * r.n[at, :], axis=0, keepdims=True)
-        r.vg[3:4, 0:D] += jnp.sum(dm, axis=0, keepdims=True)
-        r.um[at, :] = dm * row(2)
-        return 0
-
-    lax.fori_loop(0, S // QB, dm_rows, 0)
     step("i", "c", "y", "", 0)
-    step("i", "c", "y", "", 1)
-    step("o", "y", "z", "c", 0)
-    step("o", "y", "z", "c", 1)
-
-    attend(True, 0, 2)
-    send_o(0)
-    qkv_back(0)
-    step("i", "y", "z", "c", 0)
-    step("i", "y", "z", "c", 1)
-    attend(True, 2, 4)
-    send_o(1)
-    half_z = pl.ds(x * (Z // X), Z // X)
-    r.gd.reshape(D, D)[mine, :] = mm(r.ot[...], r.cots[...]).astype(BF16)
-    gd_part = r.gd.at[half_z, :, :, xo]
-    push("gd", gd_part, gd_part, at_x)
-    qkv_back(1)
-
-    def dh_rows(base, mine_too):
+
+    def input_grads(base, mine_too):
         def one(i, _):
             at = pl.ds(pl.multiple_of(base + i * QB, QB), QB)
             to = pl.ds(pl.multiple_of(i * QB, QB), QB)
+            n = r.n[at, :]
+            dm = mm(r.df[at, :], wi[...], NT)
+            r.vg[2:3, 0:D] += jnp.sum(dm * n, axis=0, keepdims=True)
+            r.vg[3:4, 0:D] += jnp.sum(dm, axis=0, keepdims=True)
             dh = mm(r.dqkv[at, :], wq[...], NT)
-            r.vg[0:1, 0:D] += jnp.sum(dh * r.n[at, :], axis=0, keepdims=True)
+            r.vg[0:1, 0:D] += jnp.sum(dh * n, axis=0, keepdims=True)
             r.vg[1:2, 0:D] += jnp.sum(dh, axis=0, keepdims=True)
-            u = dh * row(0) + r.um[at, :]
+            u = dh * row(0) + dm * row(2)
             if mine_too:
                 r.u[to, :] = u
             else:
@@ -902,11 +891,12 @@
 
         lax.fori_loop(0, T // QB, one, 0)
 
-    dh_rows(xo * T, False)
+    input_grads(xo * T, False)
     push("u", r.us, r.ur, at_x)
-    step("q", "c", "y", "", 0)
-    step("q", "c", "y", "", 1)
-    dh_rows(x * T, True)
+    step("i", "c", "y", "", 1)
+    step("q", "y", "z", "c", 0)
+    step("q", "y", "z", "c", 1)
+    input_grads(x * T, True)
 
     g_sum = jnp.sum(r.cot[...].astype(F32), axis=0, keepdims=True)
     r.vg[5:6, 0:D] = g_sum
@@ -931,8 +921,9 @@
     scatter("v", "c", "")
     wait("gd")
     scatter("d", "c", "x")
-    step("q", "y", "z", "c", 0)
-    step("q", "y", "z", "c", 1)
+    step("i", "y", "z", "c", 0)
+    r.mo[...] = mm(r.act[rows_mine, :], wo[...])
+    step("i", "y", "z", "c", 1)
 
     def flat(out, width, k=None, part=D):
         per = width // 128
@@ -945,15 +936,16 @@
 
         return put
 
+    step("v", "c", "y")
+    step("d", "c", "y", "x")
     add_parts("o", "z", "cy", 0, flat(r.oo, D, 0, CH["o"]))
     add_parts("o", "z", "cy", 1, flat(r.oo, D, 1, CH["o"]))
+    at_me = (me["z"], me["y"], me["c"])
+    step("v", "y", "z", "c")
+    step("d", "y", "z", "cx")
     add_parts("q", "z", "cy", 0)
-    add_parts("i", "z", "cy", 0)
-    add_parts("i", "z", "cy", 1)
-    at_me = (me["z"], me["y"], me["c"])
-    push("si", r.gi.at[at_me + (xo,)], r.xi, at_x)
-    step("v", "c", "y")
-    step("d", "c", "y", "x")
+    add_parts("q", "z", "cy", 1)
+    push("sq", r.gq.at[at_me + (xo,)], r.xq, at_x)
 
     wait(("o", 0))
     wait(("o", 1))
@@ -964,12 +956,11 @@
         + row(5)
         + (r.mo[...] + r.mor[...].astype(F32) + row(7))
     ).astype(BF16)
-    step("v", "y", "z", "c")
-    step("d", "y", "z", "cx")
-    add_parts("q", "z", "cy", 1)
-    push("sq", r.gq.at[at_me + (xo,)], r.xq, at_x)
     step("v", "z", "x", "cy")
     add_parts("d", "z", "cyx", None, flat(r.od, D))
+    add_parts("i", "z", "cy", 0)
+    add_parts("i", "z", "cy", 1)
+    push("si", r.gi.at[at_me + (xo,)], r.xi, at_x)
 
     wait("u")
 
@@ -1007,10 +998,10 @@
     def place_i(b):
         return b % 2, b // 4, (b // 2) % 2 == 1
 
+    wait("sq")
+    join(r.gq, r.xq, r.oq, 3 * D, place_q)
     wait("si")
     join(r.gi, r.xi, r.oi, FF, place_i)
-    wait("sq")
-    join(r.gq, r.xq, r.oq, 3 * D, place_q)
 
     def put_vec(acc):
         r.ov[...] = acc
@@ -1096,7 +1087,6 @@
     keep.of = pltpu.VMEM((D, T), BF16)
     keep.act = keep.df = pltpu.VMEM((S, FH), BF16)
     keep.slope = pltpu.VMEM((S, FH), F32)
-    keep.um = pltpu.VMEM((S, D), F32)
     keep.u = keep.mo = pltpu.VMEM((T, D), F32)
     keep.us = keep.ur = keep.mos = keep.mor = pltpu.VMEM((T, D), BF16)
     copies = 128

time: 98.1 us -> 88.8 us (0.905)
  Pallas kernels: 97.1 us -> 87.8 us
    pallas_call x1, Pallas kernels: 94.6 us -> 85.3 us  [layer(): pl.pallas_call(functools.partial(fused, sizes, names), out_shape=list(out...]
where the time goes in v4:
time: 88.8 us; the launch traced here: 88.7 us
  Pallas kernels  87.8 us (99%)
    pallas_call x1, Pallas kernels, layer(): pl.pallas_call(functools.partial(fused, sizes, names), out_shape=list(out...  85.3 us
    pallas_call x1, Pallas kernels, layer(): pl.pallas_call(hand_over, out_shape=shapes, in_specs=[vmem] * 7, out_spec...  2.5 us

profile of v4, /device:TPU:0, one launch (start us, length us, event | category | flops | bytes accessed | tf_op | source)
XLA Modules:
  0.0 88.7 jit_solution(17332577985291507364)
XLA Ops:
  0.7 85.3 %layer.1 = (bf16[512,512]{1,0:T(8,128)(2,1)}, bf16[512,512]{1,0:T(8,128)(2,1)}, f32[192,128]{1,0:T(8,128)}, f32[64,128]{1,0:T(8,128)}, f32[256,128]{1,0:T(8,128)}, /*index=5*/f32[256,128]{1,0:T(8,128)}, f32[8,128]{1,0:T(8,128)}) custom-call(bf16[512,512]{1,0:T(8,128)(2,1)} %bitcast.28, bf16[512,512]{1,0:T(8,128)(2,1)} %bitcast.29, ...), custom_call_target="tpu_custom_call" | custom-call | tf_op jit(solution)/shard_map/layer/pallas_call | solution.py:1107
  86.0 2.5 %results.1 = (bf16[512,512]{1,0:T(8,128)(2,1)}, bf16[512,512]{1,0:T(8,128)(2,1)}, f32[192,128]{1,0:T(8,128)}, f32[64,128]{1,0:T(8,128)}, f32[256,128]{1,0:T(8,12...) custom-call(bf16[512,512]{1,0:T(8,128)(2,1)} %get-tuple-element.35.r, ...), custom_call_target="tpu_custom_call" | custom-call | tf_op jit(solution)/shard_map/results/pallas_call | solution.py:1126

commit v5 on v4

--- a/solution.py
+++ b/solution.py
@@ -389,12 +389,12 @@
     Y = sizes["y"]
     Z = sizes["z"]
     N = Z * Y * C * X
-    T = r.tokens.shape[0]
+    T = held["tokens"].shape[0]
     S = T * X
     HC = HEADS // X
     HW = HC * HD
     FH = FF // X
-    CH = dict(q=384, i=FH // 2, o=D // 2)
+    CH = dict(q=384, i=FH // 2, o=D // 2, d=D // 2)
     s = lax.axis_index("seq")
     me = {"x": lax.axis_index("ctx"), "c": s % C, "y": (s // C) % Y, "z": s // (C * Y)}
     x = me["x"]
@@ -498,6 +498,16 @@
     greet = [at for a in AX for at in others(a)]
     for at in greet:
         pl.semaphore_signal(barrier, inc=1, device_id=device(at), device_id_type=MESH)
+    loads = {}
+    for k, name in enumerate(n for n in names if ("h" + n) in held):
+        loads[name] = pltpu.make_async_copy(held["h" + name], held[name], r.load.at[k])
+        loads[name].start()
+
+    def loaded(*which):
+        for name in which:
+            loads[name].wait()
+
+    loaded("fq", "fi", "fd", *["v%d" % v for v in range(8)])
 
     tmp = r.tmp
     lane = iota((1, 128), 1)
@@ -545,6 +555,7 @@
     own("wq")[...] = r.sq[x]
     own("wi")[...] = r.si[x]
 
+    loaded("tokens", "cot", "fo", "rope")
     pl.semaphore_wait(barrier, len(greet))
 
     rows_mine = pl.ds(pl.multiple_of(x * T, T), T)
@@ -581,7 +592,9 @@
     wait("sq")
     gather("q", "z", "x", 0)
     gather("q", "z", "x", 1)
-    relay("d", "x", "z", "")
+    wait(("w", "d", "x", None))
+    gather("d", "z", "x", 0)
+    gather("d", "z", "x", 1)
     wait("si")
     gather("i", "z", "x", 0)
     gather("i", "z", "x", 1)
@@ -660,17 +673,18 @@
         lax.fori_loop(0, T // RC, one, 0)
 
     affine_attn(x * T)
-    relay("d", "z", "y", "x")
+    relay("d", "z", "y", "x", 0)
     relay("q", "y", "c", "xz", 0)
     affine_mlp(x * T)
     relay("q", "y", "c", "xz", 1)
+    relay("d", "z", "y", "x", 1)
 
     wait("tok")
     norm_rows(r.tok2, xo * T, False)
     affine_attn(xo * T)
     affine_mlp(xo * T)
     relay("i", "z", "y", "x", 0)
-    relay("d", "y", "c", "xz")
+    relay("d", "y", "c", "xz", 0)
 
     wq = r.wq.reshape(D, 3 * HW)
 
@@ -695,8 +709,10 @@
 
     qkv(0)
     relay("i", "z", "y", "x", 1)
+    relay("d", "y", "c", "xz", 1)
     qkv(1)
-    arrived("d")
+    arrived("d", 0)
+    arrived("d", 1)
     wd = r.wd.reshape(D, D)
     mine = pl.ds(pl.multiple_of(x * HW, HW), HW)
     r.do2[rows_mine, :] = mm(r.cot[...], wd[mine, :], NT).astype(BF16)
@@ -759,6 +775,7 @@
     attend(False, 0, 2)
     relay("i", "y", "c", "xz", 0)
     relay("o", "z", "y", "", 0)
+    relay("o", "z", "y", "", 1)
     attend(False, 2, 4)
     relay("i", "y", "c", "xz", 1)
     r.hmt[...] = r.hm[...].T
@@ -782,7 +799,6 @@
 
     arrived("i", 0)
     lax.fori_loop(0, FH // FB // 2, ff_forward, 0)
-    relay("o", "z", "y", "", 1)
     arrived("i", 1)
     lax.fori_loop(FH // FB // 2, FH // FB, ff_forward, 0)
 
@@ -795,16 +811,20 @@
         go[at, :] = mm(r.act[:, at], r.cots[...], TN).astype(BF16)
         return 0
 
+    relay("o", "y", "c", "z", 0)
     lax.fori_loop(0, FH // FB, out_grad, 0)
     scatter("o", "c", "", 0)
     scatter("o", "c", "", 1)
-    relay("o", "y", "c", "z", 0)
+    relay("o", "y", "c", "z", 1)
 
     def send_o(b):
         own_rows = slice(b * 128, (b + 1) * 128)
         to = pl.ds(pl.multiple_of(x * HW + b * 128, 128), 128)
         push(("o", b), r.ot.at[own_rows, rows_theirs], r.of.at[to, :], at_x)
         r.of[to, :] = r.ot[own_rows, rows_mine]
+        r.gd.reshape(D, D)[to, :] = mm(r.ot[own_rows, :], r.cots[...]).astype(BF16)
+        part = r.gd.at[x * (Z // X) + b, :, :, xo]
+        push("gd", part, part, at_x)
 
     r.vg[...] = jnp.zeros_like(r.vg)
     gq = r.gq.reshape(D, 3 * HW)
@@ -834,23 +854,18 @@
             ).astype(BF16)
         scatter("q", "c", "", b)
 
-    attend(True, 0, 2)
-    relay("o", "y", "c", "z", 1)
+    attend(True, 0, 1)
+    arrived("o", 0)
+    arrived("o", 1)
+    r.mos[...] = mm(r.act[rows_theirs, :], wo[...]).astype(BF16)
+    push("mo", r.mos, r.mor, at_x)
+    attend(True, 1, 2)
     step("o", "c", "y", "", 0)
     step("o", "c", "y", "", 1)
     send_o(0)
     qkv_back(0)
-
-    arrived("o", 0)
-    arrived("o", 1)
-    r.mos[...] = mm(r.act[rows_theirs, :], wo[...]).astype(BF16)
-    push("mo", r.mos, r.mor, at_x)
     attend(True, 2, 4)
     send_o(1)
-    half_z = pl.ds(x * (Z // X), Z // X)
-    r.gd.reshape(D, D)[mine, :] = mm(r.ot[...], r.cots[...]).astype(BF16)
-    gd_part = r.gd.at[half_z, :, :, xo]
-    push("gd", gd_part, gd_part, at_x)
     step("q", "c", "y", "", 0)
     step("o", "y", "z", "c", 0)
     step("o", "y", "z", "c", 1)
@@ -892,7 +907,9 @@
         lax.fori_loop(0, T // QB, one, 0)
 
     input_grads(xo * T, False)
-    push("u", r.us, r.ur, at_x)
+    for k in range(T // QB):
+        part = slice(k * QB, (k + 1) * QB)
+        push(("u", k), r.us.at[part, :], r.ur.at[part, :], at_x)
     step("i", "c", "y", "", 1)
     step("q", "y", "z", "c", 0)
     step("q", "y", "z", "c", 1)
@@ -962,7 +979,6 @@
     add_parts("i", "z", "cy", 1)
     push("si", r.gi.at[at_me + (xo,)], r.xi, at_x)
 
-    wait("u")
 
     def final_rows(i, _):
         at = pl.ds(pl.multiple_of(i * RC, RC), RC)
@@ -973,7 +989,9 @@
         r.gtok[at, :] = (r.cot[at, :].astype(F32) + back * r.scale[at, 0:1]).astype(BF16)
         return 0
 
-    lax.fori_loop(0, T // RC, final_rows, 0)
+    for k in range(T // QB):
+        wait(("u", k))
+        lax.fori_loop(k * (QB // RC), (k + 1) * (QB // RC), final_rows, 0)
 
     def join(mine_ref, got, out, width, place):
         per = width // 128
@@ -1103,11 +1121,16 @@
         ov=jax.ShapeDtypeStruct((8, 128), F32),
     )
     vmem = pl.BlockSpec(memory_space=pltpu.VMEM)
-    names = ins + list(outs) + list(scratch)
+    shown = tokens.reshape(T, D), cotangent.reshape(T, D), *flats, jnp.asarray(rope_table(S))
+    shown += tuple(v.reshape(1, -1) for v in vectors)
+    for name, a in zip(ins, shown):
+        scratch[name] = pltpu.VMEM(a.shape, a.dtype)
+    keep.load = pltpu.SemaphoreType.DMA((len(ins),))
+    names = ["h" + n for n in ins] + list(outs) + list(scratch)
     out, gtok, gq, gd, gi, go, gv = pl.pallas_call(
         functools.partial(fused, sizes, names),
         out_shape=list(outs.values()),
-        in_specs=[vmem] * len(ins),
+        in_specs=[pl.BlockSpec(memory_space=pl.ANY)] * len(ins),
         out_specs=[vmem] * len(outs),
         scratch_shapes=list(scratch.values()),
         compiler_params=pltpu.CompilerParams(
@@ -1115,11 +1138,7 @@
         ),
         name="layer",
     )(
-        tokens.reshape(T, D),
-        cotangent.reshape(T, D),
-        *flats,
-        jnp.asarray(rope_table(S)),
-        *[v.reshape(1, -1) for v in vectors],
+        *shown
     )
     shapes = [jax.ShapeDtypeStruct(a.shape, a.dtype) for a in (out, gtok, gq, gd, gi, go)]
     shapes += [jax.ShapeDtypeStruct((1, p.shape[0]), F32) for p in vectors]

time: 88.8 us -> 88.2 us (level)
  no operation moved by 1% of the time
where the time goes in v5:
time: 88.2 us; the launch traced here: 88.1 us
  Pallas kernels  87.2 us (99%)
    pallas_call x1, Pallas kernels, layer(): pl.pallas_call(functools.partial(fused, sizes, names), out_shape=list(out...  84.7 us
    pallas_call x1, Pallas kernels, layer(): pl.pallas_call(hand_over, out_shape=shapes, in_specs=[vmem] * 7, out_spec...  2.5 us

profile of v5, /device:TPU:0, one launch (start us, length us, event | category | flops | bytes accessed | tf_op | source)
XLA Modules:
  0.0 88.1 jit_solution(2697333616751645955)
XLA Ops:
  0.7 84.7 %layer.1 = (bf16[512,512]{1,0:T(8,128)(2,1)}, bf16[512,512]{1,0:T(8,128)(2,1)}, f32[192,128]{1,0:T(8,128)}, f32[64,128]{1,0:T(8,128)}, f32[256,128]{1,0:T(8,128)}, /*index=5*/f32[256,128]{1,0:T(8,128)}, f32[8,128]{1,0:T(8,128)}) custom-call(bf16[512,512]{1,0:T(8,128)(2,1)} %bitcast.28, bf16[512,512]{1,0:T(8,128)(2,1)} %bitcast.29, ...), custom_call_target="tpu_custom_call" | custom-call | tf_op jit(solution)/shard_map/layer/pallas_call | solution.py:1130
  85.4 2.5 %results.1 = (bf16[512,512]{1,0:T(8,128)(2,1)}, bf16[512,512]{1,0:T(8,128)(2,1)}, f32[192,128]{1,0:T(8,128)}, f32[64,128]{1,0:T(8,128)}, f32[256,128]{1,0:T(8,12...) custom-call(bf16[512,512]{1,0:T(8,128)(2,1)} %get-tuple-element.35.r, ...), custom_call_target="tpu_custom_call" | custom-call | tf_op jit(solution)/shard_map/results/pallas_call | solution.py:1145

commit v6 on v5

--- a/solution.py
+++ b/solution.py
@@ -776,8 +776,6 @@
     relay("i", "y", "c", "xz", 0)
     relay("o", "z", "y", "", 0)
     relay("o", "z", "y", "", 1)
-    attend(False, 2, 4)
-    relay("i", "y", "c", "xz", 1)
     r.hmt[...] = r.hm[...].T
 
     wi = r.wi.reshape(D, FH)
@@ -799,8 +797,12 @@
 
     arrived("i", 0)
     lax.fori_loop(0, FH // FB // 2, ff_forward, 0)
+    relay("i", "y", "c", "xz", 1)
+    attend(False, 2, 3)
     arrived("i", 1)
     lax.fori_loop(FH // FB // 2, FH // FB, ff_forward, 0)
+    attend(False, 3, 4)
+    relay("o", "y", "c", "z", 0)
 
     wait("cot")
     r.cots[rows_mine, :] = r.cot[...]
@@ -811,11 +813,14 @@
         go[at, :] = mm(r.act[:, at], r.cots[...], TN).astype(BF16)
         return 0
 
-    relay("o", "y", "c", "z", 0)
+    relay("o", "y", "c", "z", 1)
+    arrived("o", 0)
+    arrived("o", 1)
+    r.mos[...] = mm(r.act[rows_theirs, :], wo[...]).astype(BF16)
+    push("mo", r.mos, r.mor, at_x)
     lax.fori_loop(0, FH // FB, out_grad, 0)
     scatter("o", "c", "", 0)
     scatter("o", "c", "", 1)
-    relay("o", "y", "c", "z", 1)
 
     def send_o(b):
         own_rows = slice(b * 128, (b + 1) * 128)
@@ -823,8 +828,20 @@
         push(("o", b), r.ot.at[own_rows, rows_theirs], r.of.at[to, :], at_x)
         r.of[to, :] = r.ot[own_rows, rows_mine]
         r.gd.reshape(D, D)[to, :] = mm(r.ot[own_rows, :], r.cots[...]).astype(BF16)
-        part = r.gd.at[x * (Z // X) + b, :, :, xo]
-        push("gd", part, part, at_x)
+        push(("gc", b), r.gd.at[x * (Z // X) + b, :, 1 - me["c"]], r.dc.at[b], others("c")[0])
+
+    def gd_y(b):
+        wait(("gc", b))
+        at = (x * (Z // X) + b, slice(None), me["c"])
+        r.gd[at] = (r.gd[at].astype(F32) + r.dc[b].astype(F32)).astype(BF16)
+        push(("gy", b), r.gd.at[at[0], 1 - me["y"], me["c"]], r.dy.at[b], others("y")[0])
+
+    def gd_x(b):
+        wait(("gy", b))
+        at = (x * (Z // X) + b, me["y"], me["c"])
+        r.gd[at] = (r.gd[at].astype(F32) + r.dy[b].astype(F32)).astype(BF16)
+        part = r.gd.at[at + (xo,)]
+        push(("gx", b), part, part, at_x)
 
     r.vg[...] = jnp.zeros_like(r.vg)
     gq = r.gq.reshape(D, 3 * HW)
@@ -854,22 +871,20 @@
             ).astype(BF16)
         scatter("q", "c", "", b)
 
-    attend(True, 0, 1)
-    arrived("o", 0)
-    arrived("o", 1)
-    r.mos[...] = mm(r.act[rows_theirs, :], wo[...]).astype(BF16)
-    push("mo", r.mos, r.mor, at_x)
-    attend(True, 1, 2)
+    attend(True, 0, 2)
     step("o", "c", "y", "", 0)
     step("o", "c", "y", "", 1)
     send_o(0)
     qkv_back(0)
     attend(True, 2, 4)
     send_o(1)
+    gd_y(0)
     step("q", "c", "y", "", 0)
     step("o", "y", "z", "c", 0)
     step("o", "y", "z", "c", 1)
     qkv_back(1)
+    gd_x(0)
+    gd_y(1)
 
     def ff_backward(b, _):
         cols = ff_cols(b)
@@ -882,6 +897,7 @@
     lax.fori_loop(0, FH // FB // 2, ff_backward, 0)
     scatter("i", "c", "", 0)
     step("q", "c", "y", "", 1)
+    gd_x(1)
     lax.fori_loop(FH // FB // 2, FH // FB, ff_backward, 0)
     scatter("i", "c", "", 1)
     step("i", "c", "y", "", 0)
@@ -936,8 +952,9 @@
     for v in range(8):
         collapse(v)
     scatter("v", "c", "")
-    wait("gd")
-    scatter("d", "c", "x")
+    wait(("gx", 0))
+    wait(("gx", 1))
+    scatter("d", "z", "cyx")
     step("i", "y", "z", "c", 0)
     r.mo[...] = mm(r.act[rows_mine, :], wo[...])
     step("i", "y", "z", "c", 1)
@@ -954,12 +971,10 @@
         return put
 
     step("v", "c", "y")
-    step("d", "c", "y", "x")
     add_parts("o", "z", "cy", 0, flat(r.oo, D, 0, CH["o"]))
     add_parts("o", "z", "cy", 1, flat(r.oo, D, 1, CH["o"]))
     at_me = (me["z"], me["y"], me["c"])
     step("v", "y", "z", "c")
-    step("d", "y", "z", "cx")
     add_parts("q", "z", "cy", 0)
     add_parts("q", "z", "cy", 1)
     push("sq", r.gq.at[at_me + (xo,)], r.xq, at_x)
@@ -1067,7 +1082,7 @@
         "o": (FF // N, D),
         "v": (8, 128),
     }
-    orders = {"q": "cyz", "d": "cyz", "i": "cyz", "o": "cyz", "v": "cyzx"}
+    orders = {"q": "cyz", "d": "z", "i": "cyz", "o": "cyz", "v": "cyzx"}
     keep = types.SimpleNamespace()
     scratch = vars(keep)
     for k, slab in slabs.items():
@@ -1076,8 +1091,10 @@
         scratch["w" + k] = pltpu.VMEM((*devs, *slab), kind)
         scratch["g" + k] = pltpu.VMEM((*devs, *slab), kind)
         for n, axis in enumerate(orders[k]):
-            done = orders[k][:n] + ("x" if k == "d" else "")
+            done = "cyx" if k == "d" else orders[k][:n]
             scratch["r" + k + axis] = parts(k, axis, done, slab, kind)
+    keep.dc = pltpu.VMEM((X, Y, X, *slabs["d"]), BF16)
+    keep.dy = pltpu.VMEM((X, X, *slabs["d"]), BF16)
     keep.xq = pltpu.VMEM(slabs["q"], BF16)
     keep.xi = pltpu.VMEM(slabs["i"], BF16)
     keep.sq = pltpu.VMEM((X, *slabs["q"]), BF16)
@@ -1170,7 +1187,7 @@
 
 def solution(mesh):
     n_seq, n_ctx = mesh.shape["seq"], mesh.shape["ctx"]
-    if n_ctx != 2 or n_seq % 8 or (D // (n_seq * n_ctx)) % 16:
+    if n_ctx != 2 or n_seq != 16 or (D // (n_seq * n_ctx)) % 16:
         return general(mesh)
     sizes = {"z": n_seq // 4, "y": 2, "c": 2, "x": n_ctx}
     flat = P(("seq", "ctx"))

time: 88.2 us -> 89.6 us (1.016)
  Pallas kernels: 87.2 us -> 88.6 us
    pallas_call x1, Pallas kernels: 84.7 us -> 86.1 us  [layer(): pl.pallas_call(functools.partial(fused, sizes, names), out_shape=list(out...]
where the time goes in v6:
time: 89.6 us; the launch traced here: 89.5 us
  Pallas kernels  88.6 us (99%)
    pallas_call x1, Pallas kernels, layer(): pl.pallas_call(functools.partial(fused, sizes, names), out_shape=list(out...  86.1 us
    pallas_call x1, Pallas kernels, layer(): pl.pallas_call(hand_over, out_shape=shapes, in_specs=[vmem] * 7, out_spec...  2.5 us

profile of v6, /device:TPU:0, one launch (start us, length us, event | category | flops | bytes accessed | tf_op | source)
XLA Modules:
  0.0 89.5 jit_solution(14795487180965617135)
XLA Ops:
  0.7 86.1 %layer.1 = (bf16[512,512]{1,0:T(8,128)(2,1)}, bf16[512,512]{1,0:T(8,128)(2,1)}, f32[192,128]{1,0:T(8,128)}, f32[64,128]{1,0:T(8,128)}, f32[256,128]{1,0:T(8,128)}, /*index=5*/f32[256,128]{1,0:T(8,128)}, f32[8,128]{1,0:T(8,128)}) custom-call(bf16[512,512]{1,0:T(8,128)(2,1)} %bitcast.28, bf16[512,512]{1,0:T(8,128)(2,1)} %bitcast.29, ...), custom_call_target="tpu_custom_call" | custom-call | tf_op jit(solution)/shard_map/layer/pallas_call | solution.py:1147
  86.8 2.5 %results.1 = (bf16[512,512]{1,0:T(8,128)(2,1)}, bf16[512,512]{1,0:T(8,128)(2,1)}, f32[192,128]{1,0:T(8,128)}, f32[64,128]{1,0:T(8,128)}, f32[256,128]{1,0:T(8,12...) custom-call(bf16[512,512]{1,0:T(8,128)(2,1)} %get-tuple-element.35.r, ...), custom_call_target="tpu_custom_call" | custom-call | tf_op jit(solution)/shard_map/results/pallas_call | solution.py:1162

commit v7 on v6

--- a/solution.py
+++ b/solution.py
@@ -776,6 +776,8 @@
     relay("i", "y", "c", "xz", 0)
     relay("o", "z", "y", "", 0)
     relay("o", "z", "y", "", 1)
+    attend(False, 2, 4)
+    relay("i", "y", "c", "xz", 1)
     r.hmt[...] = r.hm[...].T
 
     wi = r.wi.reshape(D, FH)
@@ -797,12 +799,8 @@
 
     arrived("i", 0)
     lax.fori_loop(0, FH // FB // 2, ff_forward, 0)
-    relay("i", "y", "c", "xz", 1)
-    attend(False, 2, 3)
     arrived("i", 1)
     lax.fori_loop(FH // FB // 2, FH // FB, ff_forward, 0)
-    attend(False, 3, 4)
-    relay("o", "y", "c", "z", 0)
 
     wait("cot")
     r.cots[rows_mine, :] = r.cot[...]
@@ -813,14 +811,11 @@
         go[at, :] = mm(r.act[:, at], r.cots[...], TN).astype(BF16)
         return 0
 
-    relay("o", "y", "c", "z", 1)
-    arrived("o", 0)
-    arrived("o", 1)
-    r.mos[...] = mm(r.act[rows_theirs, :], wo[...]).astype(BF16)
-    push("mo", r.mos, r.mor, at_x)
+    relay("o", "y", "c", "z", 0)
     lax.fori_loop(0, FH // FB, out_grad, 0)
     scatter("o", "c", "", 0)
     scatter("o", "c", "", 1)
+    relay("o", "y", "c", "z", 1)
 
     def send_o(b):
         own_rows = slice(b * 128, (b + 1) * 128)
@@ -871,7 +866,12 @@
             ).astype(BF16)
         scatter("q", "c", "", b)
 
-    attend(True, 0, 2)
+    attend(True, 0, 1)
+    arrived("o", 0)
+    arrived("o", 1)
+    r.mos[...] = mm(r.act[rows_theirs, :], wo[...]).astype(BF16)
+    push("mo", r.mos, r.mor, at_x)
+    attend(True, 1, 2)
     step("o", "c", "y", "", 0)
     step("o", "c", "y", "", 1)
     send_o(0)
@@ -880,8 +880,6 @@
     send_o(1)
     gd_y(0)
     step("q", "c", "y", "", 0)
-    step("o", "y", "z", "c", 0)
-    step("o", "y", "z", "c", 1)
     qkv_back(1)
     gd_x(0)
     gd_y(1)
@@ -927,6 +925,8 @@
         part = slice(k * QB, (k + 1) * QB)
         push(("u", k), r.us.at[part, :], r.ur.at[part, :], at_x)
     step("i", "c", "y", "", 1)
+    step("o", "y", "z", "c", 0)
+    step("o", "y", "z", "c", 1)
     step("q", "y", "z", "c", 0)
     step("q", "y", "z", "c", 1)
     input_grads(x * T, True)

time: 89.6 us -> 92.5 us (1.032)
  Pallas kernels: 88.6 us -> 91.5 us
    pallas_call x1, Pallas kernels: 86.1 us -> 89 us  [layer(): pl.pallas_call(functools.partial(fused, sizes, names), out_shape=list(out...]
where the time goes in v7:
time: 92.5 us; the launch traced here: 92.4 us
  Pallas kernels  91.5 us (99%)
    pallas_call x1, Pallas kernels, layer(): pl.pallas_call(functools.partial(fused, sizes, names), out_shape=list(out...  89 us
    pallas_call x1, Pallas kernels, layer(): pl.pallas_call(hand_over, out_shape=shapes, in_specs=[vmem] * 7, out_spec...  2.5 us

profile of v7, /device:TPU:0, one launch (start us, length us, event | category | flops | bytes accessed | tf_op | source)
XLA Modules:
  0.0 92.4 jit_solution(16225568827691774690)
XLA Ops:
  0.7 89.0 %layer.1 = (bf16[512,512]{1,0:T(8,128)(2,1)}, bf16[512,512]{1,0:T(8,128)(2,1)}, f32[192,128]{1,0:T(8,128)}, f32[64,128]{1,0:T(8,128)}, f32[256,128]{1,0:T(8,128)}, /*index=5*/f32[256,128]{1,0:T(8,128)}, f32[8,128]{1,0:T(8,128)}) custom-call(bf16[512,512]{1,0:T(8,128)(2,1)} %bitcast.28, bf16[512,512]{1,0:T(8,128)(2,1)} %bitcast.29, ...), custom_call_target="tpu_custom_call" | custom-call | tf_op jit(solution)/shard_map/layer/pallas_call | solution.py:1147
  89.7 2.5 %results.1 = (bf16[512,512]{1,0:T(8,128)(2,1)}, bf16[512,512]{1,0:T(8,128)(2,1)}, f32[192,128]{1,0:T(8,128)}, f32[64,128]{1,0:T(8,128)}, f32[256,128]{1,0:T(8,12...) custom-call(bf16[512,512]{1,0:T(8,128)(2,1)} %get-tuple-element.35.r, ...), custom_call_target="tpu_custom_call" | custom-call | tf_op jit(solution)/shard_map/results/pallas_call | solution.py:1162

commit v8 on v7

--- a/solution.py
+++ b/solution.py
@@ -880,6 +880,8 @@
     send_o(1)
     gd_y(0)
     step("q", "c", "y", "", 0)
+    step("o", "y", "z", "c", 0)
+    step("o", "y", "z", "c", 1)
     qkv_back(1)
     gd_x(0)
     gd_y(1)
@@ -925,8 +927,6 @@
         part = slice(k * QB, (k + 1) * QB)
         push(("u", k), r.us.at[part, :], r.ur.at[part, :], at_x)
     step("i", "c", "y", "", 1)
-    step("o", "y", "z", "c", 0)
-    step("o", "y", "z", "c", 1)
     step("q", "y", "z", "c", 0)
     step("q", "y", "z", "c", 1)
     input_grads(x * T, True)

time: 92.5 us -> 88.2 us (0.954)
  Pallas kernels: 91.5 us -> 87.2 us
    pallas_call x1, Pallas kernels: 89 us -> 84.7 us  [layer(): pl.pallas_call(functools.partial(fused, sizes, names), out_shape=list(out...]
where the time goes in v8:
time: 88.2 us; the launch traced here: 88 us
  Pallas kernels  87.2 us (99%)
    pallas_call x1, Pallas kernels, layer(): pl.pallas_call(functools.partial(fused, sizes, names), out_shape=list(out...  84.7 us
    pallas_call x1, Pallas kernels, layer(): pl.pallas_call(hand_over, out_shape=shapes, in_specs=[vmem] * 7, out_spec...  2.5 us

profile of v8, /device:TPU:0, one launch (start us, length us, event | category | flops | bytes accessed | tf_op | source)
XLA Modules:
  0.0 88.0 jit_solution(2153712738386010957)
XLA Ops:
  0.7 84.7 %layer.1 = (bf16[512,512]{1,0:T(8,128)(2,1)}, bf16[512,512]{1,0:T(8,128)(2,1)}, f32[192,128]{1,0:T(8,128)}, f32[64,128]{1,0:T(8,128)}, f32[256,128]{1,0:T(8,128)}, /*index=5*/f32[256,128]{1,0:T(8,128)}, f32[8,128]{1,0:T(8,128)}) custom-call(bf16[512,512]{1,0:T(8,128)(2,1)} %bitcast.28, bf16[512,512]{1,0:T(8,128)(2,1)} %bitcast.29, ...), custom_call_target="tpu_custom_call" | custom-call | tf_op jit(solution)/shard_map/layer/pallas_call | solution.py:1147
  85.3 2.5 %results.1 = (bf16[512,512]{1,0:T(8,128)(2,1)}, bf16[512,512]{1,0:T(8,128)(2,1)}, f32[192,128]{1,0:T(8,128)}, f32[64,128]{1,0:T(8,128)}, f32[256,128]{1,0:T(8,12...) custom-call(bf16[512,512]{1,0:T(8,128)(2,1)} %get-tuple-element.35.r, ...), custom_call_target="tpu_custom_call" | custom-call | tf_op jit(solution)/shard_map/results/pallas_call | solution.py:1162
